TPU v7x, 256 devices: a whole 4x4x8 slice. The times are simulated.
256 devices in a mesh: ocn: 8 (over z), lon: 32 (over x, y, core).
Axes of the slice: x: 4, y: 4, z: 8, core: 2. Of those that a mesh axis runs over, the one named last changes fastest.
Arguments:
- ocean_adjoint: float32 [32, 64, 4096], P(None, 'ocn', 'lon'), may hold values from -6 to 6
- mixing_coef: float32 [31, 64, 4096], P(None, 'ocn', 'lon'), may hold values from 0.05 to 20
- land_mask: int32 [64, 4096], P('ocn', 'lon'), may hold values 0 or 1
- remap_src: int32 [8, 32, 32, 2], P('ocn', 'lon'), may hold values from 0 to 7
- remap_dst: int32 [8, 32, 32, 2], P('ocn', 'lon'), may hold values from 0 to 15
- remap_live: int32 [8, 32, 32, 2], P('ocn', 'lon'), may hold values 0 or 1
- remap_weight: bfloat16 [8, 32, 32, 2, 128, 128], P('ocn', 'lon'), may hold values from -0.5 to 0.5
- atm_u: bfloat16 [64, 64, 8192], P(None, 'ocn', 'lon'), may hold values from -6 to 6
- atm_v: bfloat16 [64, 64, 8192], P(None, 'ocn', 'lon'), may hold values from -6 to 6
- spectral_nu: float32 [64], replicated, may hold values from 0.05 to 20
- band_points: int32 [8], P('ocn'), may hold values from 1284 to 5136, as said below
Outputs:
- ocean_out: float32 [32, 64, 4096], P(None, 'ocn', 'lon')
- atm_u_out: bfloat16 [64, 64, 8192], P(None, 'ocn', 'lon')
- atm_v_out: bfloat16 [64, 64, 8192], P(None, 'ocn', 'lon')
Inputs may be any that keep to these rules, and one draw needn't show every extreme that they name: `band_points`: one band has exactly 5136 points.
All inputs are finite; a program needn't handle non-finite values. No bound on the sum of `land_mask` or of `remap_live` on one device may be relied on, other than what follows from the above.
Results may differ from a plain program's by a relative error of at most 0.0059.
Values may be sent and summed in bfloat16 or wider, within the bound.
A program may use at most 256 MiB of HBM per device.

v0:
```python
import math

import jax
import jax.numpy as jnp
from jax import lax
from jax.sharding import PartitionSpec as P

K = 1280
BLK = 128


NU_MIX = 0.2


def with_halo(cells, sides, width):
    for axis, dim in sides:
        count = lax.axis_size(axis)
        ends = count - 1
        head = lax.slice_in_dim(cells, 0, width, axis=dim)
        tail = lax.slice_in_dim(cells, cells.shape[dim] - width, cells.shape[dim], axis=dim)
        cells = jnp.concatenate(
            [
                lax.ppermute(tail, axis, [(i, (i + 1) % count) for i in range(ends)]),
                cells,
                lax.ppermute(head, axis, [((i + 1) % count, i) for i in range(ends)]),
            ],
            axis=dim,
        )
    return cells


def tridiag_solve(coupling, forcing):
    flat_zero = jnp.zeros((1,) + forcing.shape[1:], jnp.float32)
    below = jnp.concatenate([flat_zero, coupling], 0)
    above = jnp.concatenate([coupling, flat_zero], 0)
    centre = 1.0 + below + above

    def forward(carried, inputs):
        ratio_prev, value_prev = carried
        below_level, centre_level, above_level, forcing_level = inputs
        pivot_value = centre_level + below_level * ratio_prev
        ratio_next = -above_level / pivot_value
        value_next = (forcing_level + below_level * value_prev) / pivot_value
        return ((ratio_next, value_next), (ratio_next, value_next))

    ignored, (ratios, values) = lax.scan(
        forward, (flat_zero[0], flat_zero[0]), (below, centre, above, forcing)
    )

    def backward(later_value, inputs):
        ratio_level, value_level = inputs
        current = value_level - ratio_level * later_value
        return (current, current)

    ignored, solution = lax.scan(backward, flat_zero[0], (ratios, values), reverse=True)
    return solution


def apply_stencil(padded, mask_pad):
    height = padded.shape[1] - 2
    width_cells = padded.shape[2] - 2
    centre = padded[:, 1:-1, 1:-1]
    flux_sum = jnp.zeros_like(centre)
    for offsets in ((0, 1), (2, 1), (1, 0), (1, 2)):
        row_off, col_off = offsets
        neighbour = padded[:, row_off : row_off + height, col_off : col_off + width_cells]
        neighbour_mask = mask_pad[row_off : row_off + height, col_off : col_off + width_cells]
        flux_sum = flux_sum + neighbour_mask[None] * (neighbour - centre)
    return mask_pad[1:-1, 1:-1][None] * (centre + NU_MIX * flux_sum)


def build_table(band_count, row_total):
    columns = jnp.arange(row_total, dtype=jnp.int32)
    wave_index = jnp.arange(K, dtype=jnp.int32)
    phase_index = columns[:, None] * wave_index[None, :] % band_count
    angles = phase_index.astype(jnp.float32) * (2.0 * math.pi) / band_count.astype(jnp.float32)
    inside = (columns < band_count).astype(jnp.float32)[:, None]
    return (jnp.concatenate([jnp.cos(angles), jnp.sin(angles)], 1) * inside).astype(jnp.bfloat16)


def finish_spectral(coeffs, viscosity, band_count, wave_table):
    wave_ratio = (jnp.arange(2 * K, dtype=jnp.int32) % K).astype(jnp.float32) / K
    damping = 1.0 / (1.0 + viscosity[:, None] * wave_ratio[None, :] * wave_ratio[None, :])
    filtered = (coeffs * damping[None, :, None, :]).astype(jnp.bfloat16)
    shape_in = filtered.shape
    grid_values = lax.dot_general(
        filtered.reshape(-1, shape_in[3]),
        wave_table,
        (((1,), (1,)), ((), ())),
        preferred_element_type=jnp.float32,
    )
    scaled = grid_values * (2.0 / band_count.astype(jnp.float32))
    return scaled.astype(jnp.bfloat16).reshape(
        shape_in[0], shape_in[1], shape_in[2], wave_table.shape[0]
    )


def back_to_grid(field_u, field_v):
    return (
        lax.all_to_all(field_u, "lon", split_axis=2, concat_axis=0, tiled=True),
        lax.all_to_all(field_v, "lon", split_axis=2, concat_axis=0, tiled=True),
    )


def per_device(
    ocean_adjoint,
    mixing_coef,
    land_mask,
    remap_src,
    remap_dst,
    remap_live,
    remap_weight,
    atm_u,
    atm_v,
    spectral_nu,
    band_points,
):
    mask_float = land_mask.astype(jnp.float32)
    solved = tridiag_solve(mixing_coef, ocean_adjoint)
    stacked = jnp.concatenate([solved, mask_float[None]], 0)
    extended = with_halo(stacked, (("ocn", 1), ("lon", 2)), 1)
    ocean_depth = solved.shape[0]
    ocean_out = apply_stencil(extended[:ocean_depth], extended[ocean_depth])
    flux_rows = ocean_out[0].astype(jnp.bfloat16)
    lon_devices = lax.axis_size("lon")
    slot_count = remap_src.shape[3]
    source_index = remap_src.reshape(lon_devices, slot_count)
    picked = flux_rows[source_index]
    weights = remap_weight.reshape(lon_devices, slot_count, BLK, BLK)
    contrib = jnp.einsum("pcab,pcb->pca", weights, picked, preferred_element_type=jnp.float32)
    live_flag = remap_live.reshape(lon_devices, slot_count)
    contrib = contrib * live_flag.astype(jnp.float32)[:, :, None]
    dest_code = jnp.where(live_flag == 1, remap_dst.reshape(lon_devices, slot_count), -1)
    levels, band_rows, lon_points = atm_u.shape
    segments = band_rows * lon_points // BLK
    segment_ids = jnp.arange(segments, dtype=jnp.int32)
    received, dest_codes = (
        lax.all_to_all(contrib, "lon", split_axis=0, concat_axis=0, tiled=True),
        lax.all_to_all(
            dest_code.astype(jnp.float32), "lon", split_axis=0, concat_axis=0, tiled=True
        ),
    )
    selector = (dest_codes[:, :, None] == segment_ids.astype(jnp.float32)[None, None, :]).astype(
        jnp.float32
    )
    surface = jnp.einsum("pcs,pca->sa", selector, received, precision=lax.Precision.HIGHEST)
    coupling = surface.reshape(band_rows, lon_points)
    lowest = (atm_u[levels - 1].astype(jnp.float32) + coupling).astype(jnp.bfloat16)
    coupled_u = jnp.concatenate([atm_u[: levels - 1], lowest[None]], 0)
    band_count = band_points[0]
    padded_lon = lon_points * lon_devices
    level_share = levels // lon_devices
    wave_table = build_table(band_count, padded_lon)
    viscosity = lax.dynamic_slice_in_dim(
        spectral_nu, lax.axis_index("lon") * level_share, level_share, 0
    )
    piece_u = lax.all_to_all(coupled_u, "lon", split_axis=0, concat_axis=2, tiled=True)
    piece_v = lax.all_to_all(atm_v, "lon", split_axis=0, concat_axis=2, tiled=True)
    both_fields = jnp.stack([piece_u, piece_v])
    coeffs = jnp.dot(
        both_fields.reshape(-1, padded_lon), wave_table, preferred_element_type=jnp.float32
    ).reshape(2, level_share, piece_u.shape[1], 2 * K)
    spectral = finish_spectral(coeffs, viscosity, band_count, wave_table)
    new_u, new_v = back_to_grid(spectral[0], spectral[1])
    return (ocean_out, new_u, new_v)


def solution(mesh):
    placed = (
        P(None, "ocn", "lon"),
        P(None, "ocn", "lon"),
        P("ocn", "lon"),
        P("ocn", "lon", None, None),
        P("ocn", "lon", None, None),
        P("ocn", "lon", None, None),
        P("ocn", "lon", None, None, None, None),
        P(None, "ocn", "lon"),
        P(None, "ocn", "lon"),
        P(),
        P("ocn"),
    )
    return jax.shard_map(
        per_device,
        mesh=mesh,
        in_specs=placed,
        out_specs=(P(None, "ocn", "lon"), P(None, "ocn", "lon"), P(None, "ocn", "lon")),
        check_vma=False,
    )
```

profile of v0, /device:TPU:97, one launch (start us, length us, event | category | flops | bytes accessed | tf_op | source)
XLA Modules:
  0.0 799.9 jit_solution(14432323375202421952)
XLA Ops:
  0.7 1.1 fusion.60
  1.8 22.4 %while.34 = (s32[]{:T(128)}, f32[8,128]{1,0:T(8,128)S(1)}, f32[8,128]{1,0:T(8,128)S(1)}, f32[32,8,128]{2,1,0:T(8,128)S(1)}, f32[32,8,128]{2,1,0:T(8,128)S(1)}, /...) while((s32[]{:T(128)}, f32[8,128]{1,0:T(8,128)S(1)}, ...), condition=%wide.region_1.2_spmd.clone, body=%wide.region_0.1_spmd.clone.sunk | while | flops 9219 | bytes 41091 | solution.py:46
  1.9 0.7 bitcast_dynamic-update-slice_fusion.5
  2.6 0.7 bitcast_dynamic-update-slice_fusion.5
  3.3 0.7 bitcast_dynamic-update-slice_fusion.5
  4.0 0.7 bitcast_dynamic-update-slice_fusion.5
  4.7 0.7 bitcast_dynamic-update-slice_fusion.5
  5.4 0.7 bitcast_dynamic-update-slice_fusion.5
  6.1 0.7 bitcast_dynamic-update-slice_fusion.5
  6.8 0.7 bitcast_dynamic-update-slice_fusion.5
  7.5 0.7 bitcast_dynamic-update-slice_fusion.5
  8.2 0.7 bitcast_dynamic-update-slice_fusion.5
  8.9 0.7 bitcast_dynamic-update-slice_fusion.5
  9.6 0.7 bitcast_dynamic-update-slice_fusion.5
  10.3 0.7 bitcast_dynamic-update-slice_fusion.5
  11.0 0.7 bitcast_dynamic-update-slice_fusion.5
  11.7 0.7 bitcast_dynamic-update-slice_fusion.5
  12.4 0.7 bitcast_dynamic-update-slice_fusion.5
  13.1 0.7 bitcast_dynamic-update-slice_fusion.5
  13.8 0.7 bitcast_dynamic-update-slice_fusion.5
  14.5 0.7 bitcast_dynamic-update-slice_fusion.5
  15.2 0.7 bitcast_dynamic-update-slice_fusion.5
  15.9 0.7 bitcast_dynamic-update-slice_fusion.5
  16.6 0.7 bitcast_dynamic-update-slice_fusion.5
  17.3 0.7 bitcast_dynamic-update-slice_fusion.5
  18.0 0.7 bitcast_dynamic-update-slice_fusion.5
  18.7 0.7 bitcast_dynamic-update-slice_fusion.5
  19.4 0.7 bitcast_dynamic-update-slice_fusion.5
  20.1 0.7 bitcast_dynamic-update-slice_fusion.5
  20.8 0.7 bitcast_dynamic-update-slice_fusion.5
  21.5 0.7 bitcast_dynamic-update-slice_fusion.5
  24.3 1.2 while.35
  26.2 1.9 collective-permute-start.1
  28.2 4.8 collective-permute-start
  32.9 0.8 fusion.55
  34.4 8.1 %all-to-all-start = ((f32[32,1,2]{2,1,0:T(1,128)}), f32[32,1,2]{2,1,0:T(1,128)S(1)}, u32[]{:S(2)}, u32[]{:S(2)}) async-start(f32[32,1,2]{2,1,0:T(1,128)} %copy.24), calls=%async_computation | async-start | bytes 32768 | tf_op jit(solution)/shard_map/all_to_all | solution.py:139
  43.9 555.2 %fusion.13 = (f32[8192,1280]{1,0:T(8,128)}, f32[8192,1280]{1,0:T(8,128)}) fusion(f32[]{:T(128)S(6)} %convert_element_type.88, pred[]{:T(512)S(6)} %lt.55, s32[]{:T(128)S(6)} %select_n.48), kind=kLoop, calls=%fused_computation.25 | loop fusion | flops 115343360 | bytes 83886088 | tf_op jit(solution)/shard_map/sin | solution.py:78
  599.1 40.9 %fusion.3 = bf16[8192,2560]{1,0:T(8,128)(2,1)} fusion(f32[8192,1280]{1,0:T(8,128)} %get-tuple-element.257, f32[8192,1280]{1,0:T(8,128)} %get-tuple-element.258, f32[8192]{0:T(1024)S(1)} %fusion.43), kind=kLoop, calls=%fused_computation.13 | loop fusion | flops 62914560 | bytes 125861888 | tf_op jit(solution)/shard_map/convert_element_type | solution.py:78
  640.3 0.9 fusion.59
  641.2 2.1 collective-permute-start.3
  643.4 3.6 collective-permute-start.2
  647.1 2.1 collective-permute-done.3
  649.2 1.3 collective-permute-done.2
  651.6 1.2 fusion.22
  652.7 0.7 broadcast_multiply_fusion
  653.5 10.2 %all-to-all-start.1 = ((f32[32,2,128]{2,1,0:T(2,128)}), f32[32,2,128]{2,1,0:T(2,128)S(1)}, u32[]{:S(2)}, u32[]{:S(2)}) async-start(f32[32,2,128]{2,1,0:T(2,128)} %broadcast_multiply_fusion), calls=%async_computation.1 | async-start | bytes 65536 | tf_op jit(solution)/shard_map/all_to_all | solution.py:138
  663.8 7.1 all-to-all-done.1
  670.9 3.9 all-to-all-start.3
  675.1 0.7 pad_maximum_fusion.1
  675.9 8.1 %all-to-all-done.3 = bf16[64,8,256]{2,1,0:T(8,128)(2,1)S(1)} async-done(((bf16[64,8,256]{2,1,0:T(8,128)(2,1)}), bf16[64,8,256]{2,1,0:T(8,128)(2,1)S(1)}, u32[]{:S(2)}, u32[]{:S(2)}) %all-to-all-start.3) | async-done | bytes 262176 | tf_op jit(solution)/shard_map/all_to_all | solution.py:158
  683.9 3.7 all-to-all-start.2
  687.8 8.9 %all-to-all-done.2 = bf16[64,8,256]{2,1,0:T(8,128)(2,1)S(1)} async-done(((bf16[64,8,256]{2,1,0:T(8,128)(2,1)}), bf16[64,8,256]{2,1,0:T(8,128)(2,1)S(1)}, u32[]{:S(2)}, u32[]{:S(2)}) %all-to-all-start.2) | async-done | bytes 262176 | tf_op jit(solution)/shard_map/all_to_all | solution.py:157
  696.8 16.5 %fusion.19 = bf16[2,2,8,2560]{3,2,1,0:T(8,128)(2,1)S(1)} fusion(bf16[8192,2560]{1,0:T(8,128)(2,1)} %fusion.3, bf16[1,2,8,8192]{3,2,1,0:T(8,128)(2,1)S(1)} %bitcast.117, bf16[1,2,8,8192]{3,2,1,0:T(8,128)(2,1)S(1)} %bitcast.118, f32[2,2560]{1,0:T(2,128)S(1)} %add_divide_fusion), kind=kOutput, calls=%fused_computation.30 | convolution fusion | flops 1342603264 | bytes 42651648 | tf_op jit(solution)/shard_map/dot_general | solution.py:160
  713.3 18.7 %fusion.15 = bf16[32,8192]{1,0:T(8,128)(2,1)S(1)} fusion(bf16[32,2560]{1,0:T(8,128)(2,1)S(1)} %bitcast.121, bf16[8192,2560]{1,0:T(8,128)(2,1)} %fusion.3, f32[]{:T(128)S(6)} %div.35), kind=kOutput, calls=%fused_computation.28 | convolution fusion | flops 1342701568 | bytes 42631172 | tf_op jit(solution)/shard_map/dot_general | solution.py:86
  732.0 6.7 copy.31
  738.8 6.4 reshape.185
  745.2 3.7 all-to-all-start.4
  748.9 6.7 copy.33
  755.7 6.4 reshape.187
  762.1 7.5 all-to-all-start.5
  769.6 5.9 reshape.186
  775.6 9.2 %copy.32 = bf16[32,2,8,256]{3,2,1,0:T(8,128)(2,1)} copy(bf16[32,2,8,256]{2,1,3,0:T(2,128)(2,1)} %bitcast.115) | data formatting | bytes 524288 | tf_op jit(solution)/shard_map/all_to_all | solution.py:100
  784.8 5.9 reshape.188
  790.7 9.2 %copy.34 = bf16[32,2,8,256]{3,2,1,0:T(8,128)(2,1)} copy(bf16[32,2,8,256]{2,1,3,0:T(2,128)(2,1)} %bitcast.116) | data formatting | bytes 524288 | tf_op jit(solution)/shard_map/all_to_all | solution.py:101
  (82 shorter events, 6.6 us)
Async XLA Ops:
  0.6 650.9 %copy-start = (bf16[1,1,32,2,128,128]{5,4,3,2,1,0:T(8,128)(2,1)S(1)}, bf16[1,1,32,2,128,128]{5,4,3,2,1,0:T(8,128)(2,1)}, u32[]{:S(2)}) copy-start(bf16[1,1,32,2,128,128]{5,4,3,2,1,0:T(8,128)(2,1)} %param.21) | copy-start | bytes 6291460
  26.2 614.0 %collective-permute-start.1 = (f32[33,1,128]{2,1,0:T(1,128)S(1)}, f32[33,1,128]{2,1,0:T(1,128)S(1)}, u32[]{:S(2)}, u32[]{:S(2)}) collective-permute-start(f32[33,1,128]{2,1,0:T(1,128)S(1)} %get-tuple-element.246), channel_id=1, source_target_pairs={{32,0},{64,32},{96,64},{128,96},{160,128},{192,160},{224,192},{33,... | collective-permute-start | bytes 50696 | tf_op jit(solution)/shard_map/ppermute | solution.py:25
  28.2 612.1 %collective-permute-start = (f32[33,1,128]{2,1,0:T(1,128)S(1)}, f32[33,1,128]{2,1,0:T(1,128)S(1)}, u32[]{:S(2)}, u32[]{:S(2)}) collective-permute-start(f32[33,1,128]{2,1,0:T(1,128)S(1)} %get-tuple-element.245), channel_id=1, source_target_pairs={{0,32},{32,64},{64,96},{96,128},{128,160},{160,192},{192,224},{1,3... | collective-permute-start | bytes 50696 | tf_op jit(solution)/shard_map/ppermute | solution.py:23
  34.4 619.1 %all-to-all-start = ((f32[32,1,2]{2,1,0:T(1,128)}), f32[32,1,2]{2,1,0:T(1,128)S(1)}, u32[]{:S(2)}, u32[]{:S(2)}) async-start(f32[32,1,2]{2,1,0:T(1,128)} %copy.24), calls=%async_computation | async-start | bytes 32768 | tf_op jit(solution)/shard_map/all_to_all | solution.py:139
  599.1 64.6 %copy-start.3 = (f32[64]{0:T(128)S(1)}, f32[64]{0:T(128)}, u32[]{:S(2)}) copy-start(f32[64]{0:T(128)} %param.24) | copy-start | bytes 772
  599.1 76.0 %copy-start.1 = (bf16[64,8,256]{2,1,0:T(8,128)(2,1)S(1)}, bf16[64,8,256]{2,1,0:T(8,128)(2,1)}, u32[]{:S(2)}) copy-start(bf16[64,8,256]{2,1,0:T(8,128)(2,1)} %param.22) | copy-start | bytes 786436
  599.1 76.0 %slice-start = ((bf16[64,8,256]{2,1,0:T(8,128)(2,1)}), bf16[63,8,256]{2,1,0:T(8,128)(2,1)S(1)}, s32[]{:S(2)}) async-start(bf16[64,8,256]{2,1,0:T(8,128)(2,1)} %param.22), calls=%async_computation.6 | async-start | bytes 516096 | tf_op jit(solution)/shard_map/slice | solution.py:149
  641.2 8.0 collective-permute-start.3
  643.4 7.1 collective-permute-start.2
  650.9 81.1 %copy-start.2 = (f32[32,8,128]{2,1,0:T(8,128)}, f32[32,8,128]{2,1,0:T(8,128)S(1)}, u32[]{:S(2)}) copy-start(f32[32,8,128]{2,1,0:T(8,128)S(1)} %fusion.32) | copy-start | bytes 393220
  653.5 17.4 %all-to-all-start.1 = ((f32[32,2,128]{2,1,0:T(2,128)}), f32[32,2,128]{2,1,0:T(2,128)S(1)}, u32[]{:S(2)}, u32[]{:S(2)}) async-start(f32[32,2,128]{2,1,0:T(2,128)} %broadcast_multiply_fusion), calls=%async_computation.1 | async-start | bytes 65536 | tf_op jit(solution)/shard_map/all_to_all | solution.py:138
  670.9 13.0 %all-to-all-start.3 = ((bf16[64,8,256]{2,1,0:T(8,128)(2,1)}), bf16[64,8,256]{2,1,0:T(8,128)(2,1)S(1)}, u32[]{:S(2)}, u32[]{:S(2)}) async-start(bf16[64,8,256]{2,1,0:T(8,128)(2,1)} %param.23), calls=%async_computation.3 | async-start | bytes 524288 | tf_op jit(solution)/shard_map/all_to_all | solution.py:158
  683.9 12.8 %all-to-all-start.2 = ((bf16[64,8,256]{2,1,0:T(8,128)(2,1)}), bf16[64,8,256]{2,1,0:T(8,128)(2,1)S(1)}, u32[]{:S(2)}, u32[]{:S(2)}) async-start(bf16[64,8,256]{2,1,0:T(8,128)(2,1)} %pad_maximum_fusion.1), calls=%async_computation.2 | async-start | bytes 524288 | tf_op jit(solution)/shard_map/all_to_all | solution.py:157
  745.2 16.9 %all-to-all-start.4 = ((bf16[32,2,2048]{2,1,0:T(2,128)(2,1)}), bf16[32,2,2048]{2,1,0:T(2,128)(2,1)S(1)}, u32[]{:S(2)}, u32[]{:S(2)}) async-start(bf16[32,2,2048]{2,1,0:T(2,128)(2,1)} %reshape.185), calls=%async_computation.4 | async-start | bytes 524288 | tf_op jit(solution)/shard_map/all_to_all | solution.py:100
  762.1 22.7 %all-to-all-start.5 = ((bf16[32,2,2048]{2,1,0:T(2,128)(2,1)}), bf16[32,2,2048]{2,1,0:T(2,128)(2,1)S(1)}, u32[]{:S(2)}, u32[]{:S(2)}) async-start(bf16[32,2,2048]{2,1,0:T(2,128)(2,1)} %reshape.187), calls=%async_computation.5 | async-start | bytes 524288 | tf_op jit(solution)/shard_map/all_to_all | solution.py:101
where the time goes:
time: 802 us; the launch traced here: 800 us
  other arithmetic  624 us (78%)
  local copies, waits for them, and re-layouts  59.5 us (7%)
  starting transfers between devices  49.5 us (6%)
  matrix products  36.6 us (5%)
  waiting for transfers between devices  27.5 us (3%)
    sin x1, other arithmetic, build_table(): jnp.sin(angles)  555 us
    convert_element_type x1, other arithmetic, build_table(): (jnp.concatenate([jnp.cos(angles), jnp.sin(angles)], 1) * inside).astype(...  40.9 us
    unnamed x12, local copies, waits for them, and re-layouts  24.8 us
    dynamic_update_slice x64, other arithmetic, tridiag_solve(): lax.scan(forward, (flat_zero[0], flat_zero[0]), (below, centre, above, fo...  22.8 us
    dot_general x1, matrix products, finish_spectral(): lax.dot_general(filtered.reshape(-1, shape_in[3]), wave_table, (((1,), (1...  18.7 us
    dot_general x1, matrix products, per_device(): jnp.dot(both_fields.reshape(-1, padded_lon), wave_table, preferred_elemen...  16.5 us
  transfers between devices with their start and end apart: 10, of which 5 were waited for; matrix products, arithmetic and copies ran while one was open for 79% of the time, Pallas kernels for 0%

commit v1 on v0

v1 whole, which is shorter than its diff:
```python
import math

import jax
import jax.numpy as jnp
from jax import lax
from jax.experimental import pallas as pl
from jax.experimental.pallas import tpu as pltpu
from jax.sharding import PartitionSpec as P

K = 1280
BLK = 128
SEGLON = 256
NBLK = 21
TWROWS = 24
KT = 256
NU_MIX = 0.2

COS_C = [(-1.0) ** m * (2.0 * math.pi) ** (2 * m) / math.factorial(2 * m) for m in range(11)]
SIN_C = [(-1.0) ** m * (2.0 * math.pi) ** (2 * m + 1) / math.factorial(2 * m + 1) for m in range(11)]


def iota(shape, dim):
    return lax.broadcasted_iota(jnp.int32, shape, dim).astype(jnp.float32)


def cos_sin(steps, points):
    inverse = 1.0 / points
    turns = jnp.floor(steps * inverse + 0.5)
    part = (steps - turns * points) * inverse
    square = part * part
    cosine = jnp.full_like(square, COS_C[10])
    sine = jnp.full_like(square, SIN_C[10])
    for m in range(9, -1, -1):
        cosine = cosine * square + COS_C[m]
        sine = sine * square + SIN_C[m]
    return cosine, sine * part


def build_tables(points, coarse, fine, coarse_t, fine_t, table, table_t, twiddle):
    n_row = jnp.full((16, K), points, jnp.float32)
    step_row, wave_row = iota((16, K), 0), iota((16, K), 1)
    coarse[0], coarse[1] = cos_sin(16.0 * step_row * wave_row, n_row)
    fine[0], fine[1] = cos_sin(step_row * wave_row, n_row)
    n_tw = jnp.full((TWROWS, K), points, jnp.float32)
    twiddle[0], twiddle[1] = cos_sin(float(SEGLON) * iota((TWROWS, K), 0) * iota((TWROWS, K), 1), n_tw)
    n_t = jnp.full((K // 16, SEGLON), points, jnp.float32)
    coarse_t[0], coarse_t[1] = cos_sin(16.0 * iota((K // 16, SEGLON), 0) * iota((K // 16, SEGLON), 1), n_t)
    n_f = jnp.full((16, SEGLON), points, jnp.float32)
    fine_t[0], fine_t[1] = cos_sin(iota((16, SEGLON), 0) * iota((16, SEGLON), 1), n_f)

    def rows(p, carry):
        cos_p, sin_p = coarse[0, pl.ds(p, 1), :], coarse[1, pl.ds(p, 1), :]
        here = pl.ds(pl.multiple_of(16 * p, 16), 16)
        table[here, 0:K] = (cos_p * fine[0] - sin_p * fine[1]).astype(jnp.bfloat16)
        table[here, K : 2 * K] = (sin_p * fine[0] + cos_p * fine[1]).astype(jnp.bfloat16)
        return carry

    lax.fori_loop(0, SEGLON // 16, rows, 0)

    def rows_t(p, carry):
        cos_p, sin_p = coarse_t[0, pl.ds(p, 1), :], coarse_t[1, pl.ds(p, 1), :]
        here = pl.ds(pl.multiple_of(16 * p, 16), 16)
        table_t[0, here, :] = (cos_p * fine_t[0] - sin_p * fine_t[1]).astype(jnp.bfloat16)
        table_t[1, here, :] = (sin_p * fine_t[0] + cos_p * fine_t[1]).astype(jnp.bfloat16)
        return carry

    lax.fori_loop(0, K // 16, rows_t, 0, unroll=2)


def spectral(rows, points, damp_rows, packed, table, table_t, twiddle, raw, spread, result):
    scale = 2.0 / jnp.full((rows, KT), points, jnp.float32)

    def tile(t, carry):
        at = pl.multiple_of(t * KT, KT)
        cos_at, sin_at = pl.ds(at, KT), pl.ds(K + at, KT)
        raw[0] = jnp.dot(packed[...], table[:, cos_at], preferred_element_type=jnp.float32)
        raw[1] = jnp.dot(packed[...], table[:, sin_at], preferred_element_type=jnp.float32)
        sum_c = jnp.zeros((rows, KT), jnp.float32)
        sum_s = jnp.zeros((rows, KT), jnp.float32)
        for l in range(NBLK):
            part_c, part_s = raw[0, l * rows : (l + 1) * rows, :], raw[1, l * rows : (l + 1) * rows, :]
            tw_c, tw_s = twiddle[0, l : l + 1, cos_at], twiddle[1, l : l + 1, cos_at]
            sum_c += tw_c * part_c - tw_s * part_s
            sum_s += tw_s * part_c + tw_c * part_s
        ratio = (iota((rows, KT), 1) + (t * KT).astype(jnp.float32)) * (1.0 / K)
        damping = scale / (1.0 + damp_rows * ratio * ratio)
        sum_c *= damping
        sum_s *= damping
        for l in range(NBLK):
            tw_c, tw_s = twiddle[0, l : l + 1, cos_at], twiddle[1, l : l + 1, cos_at]
            spread[0, l * rows : (l + 1) * rows, :] = (tw_c * sum_c + tw_s * sum_s).astype(jnp.bfloat16)
            spread[1, l * rows : (l + 1) * rows, :] = (tw_c * sum_s - tw_s * sum_c).astype(jnp.bfloat16)
        k_rows = pl.ds(at, KT)
        add = jnp.dot(spread[0], table_t[0, k_rows, :], preferred_element_type=jnp.float32)
        add += jnp.dot(spread[1], table_t[1, k_rows, :], preferred_element_type=jnp.float32)

        @pl.when(t == 0)
        def _():
            result[...] = add

        @pl.when(t > 0)
        def _():
            result[...] += add

        return carry

    lax.fori_loop(0, K // KT, tile, 0)


def spectral_kernel(n_ref, nu_ref, u_ref, v_ref, out_u, out_v, coarse, fine, coarse_t, fine_t, table, table_t, twiddle, packed, raw, spread, result):
    points = n_ref[0].astype(jnp.float32)
    build_tables(points, coarse, fine, coarse_t, fine_t, table, table_t, twiddle)
    lane = iota((16, SEGLON), 1)

    def pack(l, carry):
        inside = lane + (l * SEGLON).astype(jnp.float32) < points
        for half, ref in enumerate((u_ref, v_ref)):
            block = ref[l].astype(jnp.float32).reshape(16, SEGLON)
            packed[pl.ds(pl.multiple_of(32 * l + 16 * half, 16), 16), :] = jnp.where(inside, block, 0.0).astype(jnp.bfloat16)
        return carry

    lax.fori_loop(0, NBLK, pack, 0)
    row = iota((32, KT), 0)
    odd = ((row >= 8) & (row < 16)) | (row >= 24)
    nu = jnp.where(odd, nu_ref[1], nu_ref[0])
    spectral(32, points, nu, packed, table, table_t, twiddle, raw, spread, result)

    def unpack(l, carry):
        inside = lane + (l * SEGLON).astype(jnp.float32) < points
        for half, ref in enumerate((out_u, out_v)):
            block = result[pl.ds(pl.multiple_of(32 * l + 16 * half, 16), 16), :]
            ref[l] = jnp.where(inside, block, 0.0).reshape(2, 8, SEGLON).astype(jnp.bfloat16)
        return carry

    lax.fori_loop(0, NBLK, unpack, 0)
    for l in range(NBLK, out_u.shape[0]):
        out_u[l] = jnp.zeros_like(out_u[l])
        out_v[l] = jnp.zeros_like(out_v[l])


def spectral_call(points, nu, u, v):
    m = 32 * NBLK
    vmem = pl.BlockSpec(memory_space=pltpu.VMEM)
    smem = pl.BlockSpec(memory_space=pltpu.SMEM)
    return pl.pallas_call(
        spectral_kernel,
        out_shape=(jax.ShapeDtypeStruct(u.shape, u.dtype), jax.ShapeDtypeStruct(v.shape, v.dtype)),
        in_specs=[smem, smem, vmem, vmem],
        out_specs=(vmem, vmem),
        scratch_shapes=[
            pltpu.VMEM((2, 16, K), jnp.float32),
            pltpu.VMEM((2, 16, K), jnp.float32),
            pltpu.VMEM((2, K // 16, SEGLON), jnp.float32),
            pltpu.VMEM((2, 16, SEGLON), jnp.float32),
            pltpu.VMEM((SEGLON, 2 * K), jnp.bfloat16),
            pltpu.VMEM((2, K, SEGLON), jnp.bfloat16),
            pltpu.VMEM((2, TWROWS, K), jnp.float32),
            pltpu.VMEM((m, SEGLON), jnp.bfloat16),
            pltpu.VMEM((2, m, KT), jnp.float32),
            pltpu.VMEM((2, m, KT), jnp.bfloat16),
            pltpu.VMEM((m, SEGLON), jnp.float32),
        ],
        compiler_params=pltpu.CompilerParams(vmem_limit_bytes=40 << 20),
        name="spectral",
    )(points, nu, u, v)


def solve_kernel(mix_ref, force_ref, out_ref, ratio):
    levels = force_ref.shape[0]
    zero = jnp.zeros(force_ref.shape[1:], jnp.float32)
    rat, val, below = zero, zero, zero
    for z in range(levels - 1, -1, -1):
        above = mix_ref[z - 1] if z > 0 else zero
        inv = 1.0 / (1.0 + above + below * (1.0 - rat))
        val = (force_ref[z] + below * val) * inv
        rat = above * inv
        out_ref[z] = val
        ratio[z] = rat
        below = above
    s = out_ref[0]
    for z in range(1, levels):
        s = out_ref[z] + ratio[z] * s
        out_ref[z] = s


def solve(mix, force):
    vmem = pl.BlockSpec(memory_space=pltpu.VMEM)
    return pl.pallas_call(
        solve_kernel,
        out_shape=jax.ShapeDtypeStruct(force.shape, jnp.float32),
        in_specs=[vmem, vmem],
        out_specs=vmem,
        scratch_shapes=[pltpu.VMEM(force.shape, jnp.float32)],
        name="solve",
    )(mix, force)


def remap_kernel(src_ref, flux_ref, weight_ref, out_ref):
    def owner(p, carry):
        zero = jnp.zeros((6, BLK), jnp.float32)
        one = flux_ref[pl.ds(src_ref[2 * p], 1), :]
        two = flux_ref[pl.ds(src_ref[2 * p + 1], 1), :]
        blank = jnp.zeros((1, BLK), jnp.float32)
        left = jnp.concatenate([jnp.concatenate([one, blank], 1), jnp.concatenate([blank, two], 1)], 0)
        lhs = jnp.concatenate([left, jnp.concatenate([zero, zero], 1)], 0).astype(jnp.bfloat16)
        both = jnp.concatenate([weight_ref[p, 0], weight_ref[p, 1]], 1)
        got = lax.dot_general(lhs, both, (((1,), (1,)), ((), ())), preferred_element_type=jnp.float32)
        out_ref[p] = got[0:2]
        return carry

    lax.fori_loop(0, weight_ref.shape[0], owner, 0)


def remap(src, flux, weights):
    vmem = pl.BlockSpec(memory_space=pltpu.VMEM)
    smem = pl.BlockSpec(memory_space=pltpu.SMEM)
    return pl.pallas_call(
        remap_kernel,
        out_shape=jax.ShapeDtypeStruct((weights.shape[0], 2, BLK), jnp.float32),
        in_specs=[smem, vmem, vmem],
        out_specs=vmem,
        compiler_params=pltpu.CompilerParams(vmem_limit_bytes=20 << 20),
        name="remap",
    )(src, flux, weights)


def with_halo(cells, sides, width):
    for axis, dim in sides:
        count = lax.axis_size(axis)
        ends = count - 1
        head = lax.slice_in_dim(cells, 0, width, axis=dim)
        tail = lax.slice_in_dim(cells, cells.shape[dim] - width, cells.shape[dim], axis=dim)
        cells = jnp.concatenate(
            [
                lax.ppermute(tail, axis, [(i, (i + 1) % count) for i in range(ends)]),
                cells,
                lax.ppermute(head, axis, [((i + 1) % count, i) for i in range(ends)]),
            ],
            axis=dim,
        )
    return cells


def apply_stencil(padded, mask_pad):
    height = padded.shape[1] - 2
    width_cells = padded.shape[2] - 2
    centre = padded[:, 1:-1, 1:-1]
    flux_sum = jnp.zeros_like(centre)
    for offsets in ((0, 1), (2, 1), (1, 0), (1, 2)):
        row_off, col_off = offsets
        neighbour = padded[:, row_off : row_off + height, col_off : col_off + width_cells]
        neighbour_mask = mask_pad[row_off : row_off + height, col_off : col_off + width_cells]
        flux_sum = flux_sum + neighbour_mask[None] * (neighbour - centre)
    return mask_pad[1:-1, 1:-1][None] * (centre + NU_MIX * flux_sum)


def per_device(
    ocean_adjoint,
    mixing_coef,
    land_mask,
    remap_src,
    remap_dst,
    remap_live,
    remap_weight,
    atm_u,
    atm_v,
    spectral_nu,
    band_points,
):
    lon_devices = lax.axis_size("lon")
    levels, band_rows, lon_points = atm_u.shape
    share = levels // lon_devices
    swap = lambda x: lax.all_to_all(x, "lon", split_axis=0, concat_axis=0, tiled=True)
    piece_v = swap(atm_v.reshape(lon_devices, share, band_rows, lon_points))
    mask_float = land_mask.astype(jnp.float32)
    solved = solve(mixing_coef, ocean_adjoint)
    stacked = jnp.concatenate([solved, mask_float[None]], 0)
    extended = with_halo(stacked, (("ocn", 1), ("lon", 2)), 1)
    ocean_depth = solved.shape[0]
    ocean_out = apply_stencil(extended[:ocean_depth], extended[ocean_depth])
    slot_count = remap_src.shape[3]
    weights = remap_weight.reshape(lon_devices, slot_count, BLK, BLK)
    flux = ocean_out[0].astype(jnp.bfloat16).astype(jnp.float32)
    contrib = remap(remap_src.reshape(-1), flux, weights)
    live = remap_live.reshape(lon_devices, slot_count)
    contrib = contrib * live.astype(jnp.float32)[:, :, None]
    code = jnp.where(live == 1, remap_dst.reshape(lon_devices, slot_count), -1).astype(jnp.float32)
    codes = jnp.broadcast_to(code[:, :, None], contrib.shape)
    both = swap(jnp.concatenate([contrib, codes], 1))
    received, dest = both[:, :slot_count], both[:, slot_count:, 0]
    segments = band_rows * lon_points // BLK
    selector = (dest[:, :, None] == jnp.arange(segments).astype(jnp.float32)).astype(jnp.float32)
    surface = jnp.einsum("pcs,pca->sa", selector, received, precision=lax.Precision.HIGHEST)
    lowest = (atm_u[levels - 1].astype(jnp.float32) + surface.reshape(band_rows, lon_points)).astype(jnp.bfloat16)
    coupled_u = jnp.concatenate([atm_u[: levels - 1], lowest[None]], 0)
    piece_u = swap(coupled_u.reshape(lon_devices, share, band_rows, lon_points))
    nu = lax.dynamic_slice_in_dim(spectral_nu, lax.axis_index("lon") * share, share, 0)
    new_u, new_v = spectral_call(band_points, nu, piece_u, piece_v)
    return (ocean_out, swap(new_u).reshape(atm_u.shape), swap(new_v).reshape(atm_v.shape))


def solution(mesh):
    placed = (
        P(None, "ocn", "lon"),
        P(None, "ocn", "lon"),
        P("ocn", "lon"),
        P("ocn", "lon", None, None),
        P("ocn", "lon", None, None),
        P("ocn", "lon", None, None),
        P("ocn", "lon", None, None, None, None),
        P(None, "ocn", "lon"),
        P(None, "ocn", "lon"),
        P(),
        P("ocn"),
    )
    return jax.shard_map(
        per_device,
        mesh=mesh,
        in_specs=placed,
        out_specs=(P(None, "ocn", "lon"), P(None, "ocn", "lon"), P(None, "ocn", "lon")),
        check_vma=False,
    )
```

time: 802 us -> 113 us (0.14)
  other arithmetic: 624 us -> 5.36 us
  local copies, waits for them, and re-layouts: 59.5 us -> 2.31 us
  matrix products: 36.6 us -> 0.26 us
  starting transfers between devices: 49.5 us -> 33.5 us
  Pallas kernels: 0 us -> 15.9 us
  waiting for transfers between devices: 27.5 us -> 41.2 us
  blocking collectives: 0 us -> 12.4 us
    sin x1 -> x0, other arithmetic: 555 us -> none  [build_table(): jnp.sin(angles)]
    convert_element_type x5 -> x4, other arithmetic: 41.7 us -> 0.77 us  [the longest x1 0.76 us: per_device(): contrib = contrib * live.astype(jnp.float32)[:, :, None]]
    dot_general x3 -> x0, matrix products: 36.4 us -> none  [the longest x1 18.7 us: finish_spectral(): lax.dot_general(filtered.reshape(-1, shape_in[3]), wave_table, (((1,), (1...]
    unnamed x12 -> x15, local copies, waits for them, and re-layouts: 24.8 us -> 1.52 us
    dynamic_update_slice x64 -> x0, other arithmetic: 22.8 us -> none  [tridiag_solve(): lax.scan(forward, (flat_zero[0], flat_zero[0]), (below, centre, above, fo...]
    all_to_all x5 -> x0, local copies, waits for them, and re-layouts: 18.5 us -> none  [the longest x1 9.22 us: back_to_grid(): lax.all_to_all(field_u, 'lon', split_axis=2, concat_axis=0, tiled=True)]
    all_to_all x6 -> x4, starting transfers between devices: 37.1 us -> 19.7 us  [per_device(): lax.all_to_all(x, 'lon', split_axis=0, concat_axis=0, tiled=True)]
    pallas_call x0 -> x3, Pallas kernels: none -> 15.9 us  [the longest x1 8.42 us: spectral_call(): pl.pallas_call(spectral_kernel, out_shape=(jax.ShapeDtypeStruct(u.shape,...]
  transfers between devices with their start and end apart: 10 -> 8, of which waited for: 5 -> 7; matrix products, arithmetic and copies ran while one was open for 79% -> 2% of each run, Pallas kernels for 0% -> 0%
where the time goes in v1:
time: 113 us
  waiting for transfers between devices  41.2 us (36%)
  starting transfers between devices  33.5 us (30%)
  Pallas kernels  15.9 us (14%)
  blocking collectives  12.4 us (11%)
  other arithmetic  5.36 us (5%)
  local copies, waits for them, and re-layouts  2.31 us (2%)
  between operations  1.5 us (1%)
    all_to_all x4, waiting for transfers between devices, per_device(): lax.all_to_all(x, 'lon', split_axis=0, concat_axis=0, tiled=True)  32.7 us
    all_to_all x4, starting transfers between devices, per_device(): lax.all_to_all(x, 'lon', split_axis=0, concat_axis=0, tiled=True)  19.7 us
    all_to_all x1, blocking collectives, per_device(): lax.all_to_all(x, 'lon', split_axis=0, concat_axis=0, tiled=True)  12.4 us
    ppermute x2, starting transfers between devices, with_halo(): lax.ppermute(tail, axis, [(i, (i + 1) % count) for i in range(ends)])  9.95 us
    pallas_call x1, Pallas kernels, spectral_call(): pl.pallas_call(spectral_kernel, out_shape=(jax.ShapeDtypeStruct(u.shape,...  8.42 us
    ppermute x2, waiting for transfers between devices, with_halo(): lax.ppermute(head, axis, [((i + 1) % count, i) for i in range(ends)])  8.16 us
    pallas_call x1, Pallas kernels, remap(): pl.pallas_call(remap_kernel, out_shape=jax.ShapeDtypeStruct((weights.shap...  5.32 us
    ppermute x2, starting transfers between devices, with_halo(): lax.ppermute(head, axis, [((i + 1) % count, i) for i in range(ends)])  3.84 us
  transfers between devices with their start and end apart: 8, of which 7 were waited for; matrix products, arithmetic and copies ran while one was open for 2% of the time, Pallas kernels for 0%

profile of v1, /device:TPU:97, one launch (start us, length us, event | category | flops | bytes accessed | tf_op | source)
XLA Modules:
  0.0 112.5 jit_solution(14964777496023433688)
XLA Ops:
  0.6 0.0 copy-start.4
  0.6 0.7 convert_bitcast_fusion
  1.3 0.0 copy-start
  1.3 2.2 %solve.1 = f32[32,8,128]{2,1,0:T(8,128)} custom-call(f32[31,8,128]{2,1,0:T(8,128)} %mix_ref.1, f32[32,8,128]{2,1,0:T(8,128)} %force_ref.1), custom_call_target="tpu_custom_call" | custom-call | tf_op jit(solution)/shard_map/solve/pallas_call | solution.py:188
  3.5 0.0 copy-start.1
  3.5 1.1 pad_maximum_fusion.16
  4.6 4.8 %collective-permute-start = (f32[33,1,128]{2,1,0:T(1,128)S(1)}, f32[33,1,128]{2,1,0:T(1,128)S(1)}, u32[]{:S(2)}, u32[]{:S(2)}) collective-permute-start(f32[33,1,128]{2,1,0:T(1,128)S(1)} %get-tuple-element.9), channel_id=1, source_target_pairs={{0,32},{32,64},{64,96},{96,128},{128,160},{160,192},{192,224},{1,3... | collective-permute-start | bytes 50696 | tf_op jit(solution)/shard_map/ppermute | solution.py:235
  9.3 1.9 %collective-permute-start.1 = (f32[33,1,128]{2,1,0:T(1,128)S(1)}, f32[33,1,128]{2,1,0:T(1,128)S(1)}, u32[]{:S(2)}, u32[]{:S(2)}) collective-permute-start(f32[33,1,128]{2,1,0:T(1,128)S(1)} %get-tuple-element.10), channel_id=1, source_target_pairs={{32,0},{64,32},{96,64},{128,96},{160,128},{192,160},{224,192},{33,... | collective-permute-start | bytes 50696 | tf_op jit(solution)/shard_map/ppermute | solution.py:237
  11.3 0.0 collective-permute-done
  11.3 3.8 %collective-permute-done.1 = f32[33,1,128]{2,1,0:T(1,128)S(1)} collective-permute-done((f32[33,1,128]{2,1,0:T(1,128)S(1)}, f32[33,1,128]{2,1,0:T(1,128)S(1)}, u32[]{:S(2)}, u32[]{:S(2)}) %collective-permute-start.1) | collective-permute-done | bytes 16928 | tf_op jit(solution)/shard_map/ppermute | solution.py:237
  15.0 1.0 pad_maximum_fusion
  16.0 0.1 fusion.23
  16.1 5.2 %collective-permute-start.2 = (f32[33,10,1]{2,1,0:T(8,128)S(1)}, f32[33,10,1]{2,1,0:T(8,128)S(1)}, u32[]{:S(2)}, u32[]{:S(2)}) collective-permute-start(f32[33,10,1]{2,1,0:T(8,128)S(1)} %get-tuple-element.7), channel_id=1, source_target_pairs={{0,1},{1,2},{2,3},{3,4},{4,5},{5,6},{6,7},{7,8},{8,9},{9,10},{10,1... | collective-permute-start | bytes 3968 | tf_op jit(solution)/shard_map/ppermute | solution.py:235
  21.3 1.9 %collective-permute-start.3 = (f32[33,10,1]{2,1,0:T(8,128)S(1)}, f32[33,10,1]{2,1,0:T(8,128)S(1)}, u32[]{:S(2)}, u32[]{:S(2)}) collective-permute-start(f32[33,10,1]{2,1,0:T(8,128)S(1)} %get-tuple-element.8), channel_id=1, source_target_pairs={{1,0},{2,1},{3,2},{4,3},{5,4},{6,5},{7,6},{8,7},{9,8},{10,9},{11,1... | collective-permute-start | bytes 3968 | tf_op jit(solution)/shard_map/ppermute | solution.py:237
  23.3 0.8 convert_bitcast_fusion.1
  24.0 0.0 copy-done.4
  24.0 0.1 copy.19
  24.1 0.1 reshape.64.src_ref
  24.2 0.1 copy.20
  24.3 0.1 copy.21
  24.4 0.3 collective-permute-done.2
  24.7 4.4 %collective-permute-done.3 = f32[33,10,1]{2,1,0:T(8,128)S(1)} collective-permute-done((f32[33,10,1]{2,1,0:T(8,128)S(1)}, f32[33,10,1]{2,1,0:T(8,128)S(1)}, u32[]{:S(2)}, u32[]{:S(2)}) %collective-permute-start.3) | collective-permute-done | bytes 1352 | tf_op jit(solution)/shard_map/ppermute | solution.py:237
  29.1 0.0 copy-done.1
  29.1 0.1 fusion.15
  29.2 0.1 fusion.24
  29.3 0.0 copy-start.2
  29.3 0.0 slice-start
  29.3 0.3 fusion.5
  29.5 0.0 copy-start.3
  29.6 0.0 copy-done
  29.6 0.0 copy-start.5
  29.6 5.3 %remap.1 = f32[32,2,128]{2,1,0:T(2,128)S(1)} custom-call(s32[64]{0:T(128)S(1)} %reshape.64.src_ref, f32[8,128]{1,0:T(8,128)S(1)} %fusion.20.flux_ref, bf16[32,2,128,128]{3,2,1,0:T(8,128)(2,1)S(1)} %bitcast.23), custom_call_target="tpu_custom_call" | custom-call | tf_op jit(solution)/shard_map/remap/pallas_call | solution.py:217
  34.9 0.1 broadcast_multiply_fusion
  35.0 0.1 broadcast_in_dim.10
  35.1 0.7 pad_maximum_fusion.14
  35.8 8.4 %all-to-all-start = ((f32[32,4,128]{2,1,0:T(4,128)}), f32[32,4,128]{2,1,0:T(4,128)S(1)}, u32[]{:S(2)}, u32[]{:S(2)}) async-start(f32[32,4,128]{2,1,0:T(4,128)} %pad_maximum_fusion.14), calls=%async_computation | async-start | bytes 131072 | tf_op jit(solution)/shard_map/all_to_all | solution.py:273
  44.2 7.4 %all-to-all-done = f32[32,4,128]{2,1,0:T(4,128)S(1)} async-done(((f32[32,4,128]{2,1,0:T(4,128)}), f32[32,4,128]{2,1,0:T(4,128)S(1)}, u32[]{:S(2)}, u32[]{:S(2)}) %all-to-all-start) | async-done | bytes 65568 | tf_op jit(solution)/shard_map/all_to_all | solution.py:273
  51.6 3.9 %all-to-all-start.2 = ((bf16[32,2,8,256]{3,2,1,0:T(8,128)(2,1)}), bf16[32,2,8,256]{3,2,1,0:T(8,128)(2,1)S(1)}, u32[]{:S(2)}, u32[]{:S(2)}) async-start(bf16[32,2,8,256]{3,2,1,0:T(8,128)(2,1)} %bitcast.9), calls=%async_computation.2 | async-start | bytes 524288 | tf_op jit(solution)/shard_map/all_to_all | solution.py:273
  55.5 0.1 copy.22
  55.6 0.3 convolution_bitcast_fusion
  55.9 0.0 copy-done.2
  55.9 0.0 slice-done
  55.9 0.7 pad_maximum_fusion.1
  56.7 7.9 %all-to-all-done.2.v_ref = bf16[32,2,8,256]{3,2,1,0:T(8,128)(2,1)S(1)} async-done(((bf16[32,2,8,256]{3,2,1,0:T(8,128)(2,1)}), bf16[32,2,8,256]{3,2,1,0:T(8,128)(2,1)S(1)}, u32[]{:S(2)}, u32[]{:S(2)}) %all-to-all-start.2) | async-done | bytes 262176 | tf_op jit(solution)/shard_map/all_to_all | solution.py:273
  64.6 0.0 copy-done.3
  64.6 3.7 %all-to-all-start.1 = ((bf16[32,2,8,256]{3,2,1,0:T(8,128)(2,1)}), bf16[32,2,8,256]{3,2,1,0:T(8,128)(2,1)S(1)}, u32[]{:S(2)}, u32[]{:S(2)}) async-start(bf16[32,2,8,256]{3,2,1,0:T(8,128)(2,1)} %bitcast.8), calls=%async_computation.1 | async-start | bytes 524288 | tf_op jit(solution)/shard_map/all_to_all | solution.py:273
  69.0 0.0 copy-done.5
  69.0 0.1 dynamic_slice.3.nu_ref
  69.1 8.4 %all-to-all-done.1.u_ref = bf16[32,2,8,256]{3,2,1,0:T(8,128)(2,1)S(1)} async-done(((bf16[32,2,8,256]{3,2,1,0:T(8,128)(2,1)}), bf16[32,2,8,256]{3,2,1,0:T(8,128)(2,1)S(1)}, u32[]{:S(2)}, u32[]{:S(2)}) %all-to-all-start.1) | async-done | bytes 262176 | tf_op jit(solution)/shard_map/all_to_all | solution.py:273
  77.4 8.4 %spectral.1 = (bf16[32,2,8,256]{3,2,1,0:T(8,128)(2,1)S(1)}, bf16[32,2,8,256]{3,2,1,0:T(8,128)(2,1)}) custom-call(s32[1]{0:T(128)S(6)} %copy.28.n_ref, f32[2]{0:T(128)S(1)} %dynamic_slice.3.nu_ref, bf16[32,2,8,256]{3,2,1,0:T(8,128)(2,1)S(1)} %all-to-all-done.1.u_ref, bf16[32,2,8,256]{3,2,1,0:T(8,128)(2,1)S(1)} %all-to-all-done.2.v_ref), custom_call_target="tpu_custom_call" | custom-call | tf_op jit(solution)/shard_map/spectral/pallas_call | solution.py:145
  85.8 12.4 %all_to_all.25 = bf16[32,2,8,256]{3,2,1,0:T(8,128)(2,1)S(1)} all-to-all(bf16[32,2,8,256]{3,2,1,0:T(8,128)(2,1)S(1)} %get-tuple-element.5), channel_id=1, replica_groups=mesh['ocn'=8,'lon'=32] {'lon'}, dimensions={0} | all-to-all | bytes 524288 | tf_op jit(solution)/shard_map/all_to_all | solution.py:273
  98.3 3.7 %all-to-all-start.4 = ((bf16[32,2,8,256]{3,2,1,0:T(8,128)(2,1)}), bf16[32,2,8,256]{3,2,1,0:T(8,128)(2,1)S(1)}, u32[]{:S(2)}, u32[]{:S(2)}) async-start(bf16[32,2,8,256]{3,2,1,0:T(8,128)(2,1)} %get-tuple-element.6), calls=%async_computation.4 | async-start | bytes 524288 | tf_op jit(solution)/shard_map/all_to_all | solution.py:273
  102.0 9.1 %all-to-all-done.4 = bf16[32,2,8,256]{3,2,1,0:T(8,128)(2,1)S(1)} async-done(((bf16[32,2,8,256]{3,2,1,0:T(8,128)(2,1)}), bf16[32,2,8,256]{3,2,1,0:T(8,128)(2,1)S(1)}, u32[]{:S(2)}, u32[]{:S(2)}) %all-to-all-start.4) | async-done | bytes 262176 | tf_op jit(solution)/shard_map/all_to_all | solution.py:273
  111.1 0.7 copy.29
  111.8 0.7 copy.30
  (6 shorter events, 0.1 us)
Async XLA Ops:
  0.6 23.4 %copy-start.4 = (s32[1,1,32,2]{2,3,1,0:T(2,128)S(1)}, s32[1,1,32,2]{2,3,1,0:T(2,128)}, u32[]{:S(2)}) copy-start(s32[1,1,32,2]{2,3,1,0:T(2,128)} %param.14) | copy-start | bytes 772
  1.3 28.2 %copy-start = (bf16[1,1,32,2,128,128]{5,4,3,2,1,0:T(8,128)(2,1)S(1)}, bf16[1,1,32,2,128,128]{5,4,3,2,1,0:T(8,128)(2,1)}, u32[]{:S(2)}) copy-start(bf16[1,1,32,2,128,128]{5,4,3,2,1,0:T(8,128)(2,1)} %param.17) | copy-start | bytes 6291460
  3.5 25.6 %copy-start.1 = (f32[32,8,128]{2,1,0:T(8,128)S(1)}, f32[32,8,128]{2,1,0:T(8,128)}, u32[]{:S(2)}) copy-start(f32[32,8,128]{2,1,0:T(8,128)} %solve.1) | copy-start | bytes 393220
  4.6 6.7 %collective-permute-start = (f32[33,1,128]{2,1,0:T(1,128)S(1)}, f32[33,1,128]{2,1,0:T(1,128)S(1)}, u32[]{:S(2)}, u32[]{:S(2)}) collective-permute-start(f32[33,1,128]{2,1,0:T(1,128)S(1)} %get-tuple-element.9), channel_id=1, source_target_pairs={{0,32},{32,64},{64,96},{96,128},{128,160},{160,192},{192,224},{1,3... | collective-permute-start | bytes 50696 | tf_op jit(solution)/shard_map/ppermute | solution.py:235
  9.3 5.7 %collective-permute-start.1 = (f32[33,1,128]{2,1,0:T(1,128)S(1)}, f32[33,1,128]{2,1,0:T(1,128)S(1)}, u32[]{:S(2)}, u32[]{:S(2)}) collective-permute-start(f32[33,1,128]{2,1,0:T(1,128)S(1)} %get-tuple-element.10), channel_id=1, source_target_pairs={{32,0},{64,32},{96,64},{128,96},{160,128},{192,160},{224,192},{33,... | collective-permute-start | bytes 50696 | tf_op jit(solution)/shard_map/ppermute | solution.py:237
  16.1 8.6 %collective-permute-start.2 = (f32[33,10,1]{2,1,0:T(8,128)S(1)}, f32[33,10,1]{2,1,0:T(8,128)S(1)}, u32[]{:S(2)}, u32[]{:S(2)}) collective-permute-start(f32[33,10,1]{2,1,0:T(8,128)S(1)} %get-tuple-element.7), channel_id=1, source_target_pairs={{0,1},{1,2},{2,3},{3,4},{4,5},{5,6},{6,7},{7,8},{8,9},{9,10},{10,1... | collective-permute-start | bytes 3968 | tf_op jit(solution)/shard_map/ppermute | solution.py:235
  21.3 7.8 %collective-permute-start.3 = (f32[33,10,1]{2,1,0:T(8,128)S(1)}, f32[33,10,1]{2,1,0:T(8,128)S(1)}, u32[]{:S(2)}, u32[]{:S(2)}) collective-permute-start(f32[33,10,1]{2,1,0:T(8,128)S(1)} %get-tuple-element.8), channel_id=1, source_target_pairs={{1,0},{2,1},{3,2},{4,3},{5,4},{6,5},{7,6},{8,7},{9,8},{10,9},{11,1... | collective-permute-start | bytes 3968 | tf_op jit(solution)/shard_map/ppermute | solution.py:237
  29.3 26.6 %copy-start.2 = (bf16[64,8,256]{2,1,0:T(8,128)(2,1)S(1)}, bf16[64,8,256]{2,1,0:T(8,128)(2,1)}, u32[]{:S(2)}) copy-start(bf16[64,8,256]{2,1,0:T(8,128)(2,1)} %param.18) | copy-start | bytes 786436
  29.3 26.7 %slice-start = ((bf16[64,8,256]{2,1,0:T(8,128)(2,1)}), bf16[63,8,256]{2,1,0:T(8,128)(2,1)S(1)}, s32[]{:S(2)}) async-start(bf16[64,8,256]{2,1,0:T(8,128)(2,1)} %param.18), calls=%async_computation.5 | async-start | bytes 516096 | tf_op jit(solution)/shard_map/slice | solution.py:295
  29.5 35.1 %copy-start.3 = (f32[32,8,128]{2,1,0:T(8,128)}, f32[32,8,128]{2,1,0:T(8,128)S(1)}, u32[]{:S(2)}) copy-start(f32[32,8,128]{2,1,0:T(8,128)S(1)} %fusion.5) | copy-start | bytes 393220
  29.6 39.4 %copy-start.5 = (f32[64]{0:T(128)S(1)}, f32[64]{0:T(128)}, u32[]{:S(2)}) copy-start(f32[64]{0:T(128)} %param.20) | copy-start | bytes 772
  35.8 15.8 %all-to-all-start = ((f32[32,4,128]{2,1,0:T(4,128)}), f32[32,4,128]{2,1,0:T(4,128)S(1)}, u32[]{:S(2)}, u32[]{:S(2)}) async-start(f32[32,4,128]{2,1,0:T(4,128)} %pad_maximum_fusion.14), calls=%async_computation | async-start | bytes 131072 | tf_op jit(solution)/shard_map/all_to_all | solution.py:273
  51.6 13.0 %all-to-all-start.2 = ((bf16[32,2,8,256]{3,2,1,0:T(8,128)(2,1)}), bf16[32,2,8,256]{3,2,1,0:T(8,128)(2,1)S(1)}, u32[]{:S(2)}, u32[]{:S(2)}) async-start(bf16[32,2,8,256]{3,2,1,0:T(8,128)(2,1)} %bitcast.9), calls=%async_computation.2 | async-start | bytes 524288 | tf_op jit(solution)/shard_map/all_to_all | solution.py:273
  64.6 12.8 %all-to-all-start.1 = ((bf16[32,2,8,256]{3,2,1,0:T(8,128)(2,1)}), bf16[32,2,8,256]{3,2,1,0:T(8,128)(2,1)S(1)}, u32[]{:S(2)}, u32[]{:S(2)}) async-start(bf16[32,2,8,256]{3,2,1,0:T(8,128)(2,1)} %bitcast.8), calls=%async_computation.1 | async-start | bytes 524288 | tf_op jit(solution)/shard_map/all_to_all | solution.py:273
  98.3 12.8 %all-to-all-start.4 = ((bf16[32,2,8,256]{3,2,1,0:T(8,128)(2,1)}), bf16[32,2,8,256]{3,2,1,0:T(8,128)(2,1)S(1)}, u32[]{:S(2)}, u32[]{:S(2)}) async-start(bf16[32,2,8,256]{3,2,1,0:T(8,128)(2,1)} %get-tuple-element.6), calls=%async_computation.4 | async-start | bytes 524288 | tf_op jit(solution)/shard_map/all_to_all | solution.py:273

commit v2 on v1

v2 whole, which is shorter than its diff:
```python
import math

import jax
import jax.numpy as jnp
from jax import lax
from jax.experimental import pallas as pl
from jax.experimental.pallas import tpu as pltpu
from jax.sharding import PartitionSpec as P

K = 1280
BLK = 128
SEGLON = 256
NBLK = 21
TWROWS = 24
KT = 256
NU_MIX = 0.2
MESH = pl.DeviceIdType.MESH

COS_C = [(-1.0) ** m * (2.0 * math.pi) ** (2 * m) / math.factorial(2 * m) for m in range(11)]
SIN_C = [(-1.0) ** m * (2.0 * math.pi) ** (2 * m + 1) / math.factorial(2 * m + 1) for m in range(11)]


def iota(shape, dim):
    return lax.broadcasted_iota(jnp.int32, shape, dim).astype(jnp.float32)


def cos_sin(steps, points):
    inverse = 1.0 / points
    turns = jnp.floor(steps * inverse + 0.5)
    part = (steps - turns * points) * inverse
    square = part * part
    cosine = jnp.full_like(square, COS_C[10])
    sine = jnp.full_like(square, SIN_C[10])
    for m in range(9, -1, -1):
        cosine = cosine * square + COS_C[m]
        sine = sine * square + SIN_C[m]
    return cosine, sine * part


def build_tables(points, coarse, fine, coarse_t, fine_t, table, table_t, twiddle):
    n_row = jnp.full((16, K), points, jnp.float32)
    step_row, wave_row = iota((16, K), 0), iota((16, K), 1)
    coarse[0], coarse[1] = cos_sin(16.0 * step_row * wave_row, n_row)
    fine[0], fine[1] = cos_sin(step_row * wave_row, n_row)
    n_tw = jnp.full((TWROWS, K), points, jnp.float32)
    twiddle[0], twiddle[1] = cos_sin(float(SEGLON) * iota((TWROWS, K), 0) * iota((TWROWS, K), 1), n_tw)
    n_t = jnp.full((K // 16, SEGLON), points, jnp.float32)
    coarse_t[0], coarse_t[1] = cos_sin(16.0 * iota((K // 16, SEGLON), 0) * iota((K // 16, SEGLON), 1), n_t)
    n_f = jnp.full((16, SEGLON), points, jnp.float32)
    fine_t[0], fine_t[1] = cos_sin(iota((16, SEGLON), 0) * iota((16, SEGLON), 1), n_f)

    def rows(p, carry):
        cos_p, sin_p = coarse[0, pl.ds(p, 1), :], coarse[1, pl.ds(p, 1), :]
        here = pl.ds(pl.multiple_of(16 * p, 16), 16)
        table[here, 0:K] = (cos_p * fine[0] - sin_p * fine[1]).astype(jnp.bfloat16)
        table[here, K : 2 * K] = (sin_p * fine[0] + cos_p * fine[1]).astype(jnp.bfloat16)
        return carry

    lax.fori_loop(0, SEGLON // 16, rows, 0)

    def rows_t(p, carry):
        cos_p, sin_p = coarse_t[0, pl.ds(p, 1), :], coarse_t[1, pl.ds(p, 1), :]
        here = pl.ds(pl.multiple_of(16 * p, 16), 16)
        table_t[0, here, :] = (cos_p * fine_t[0] - sin_p * fine_t[1]).astype(jnp.bfloat16)
        table_t[1, here, :] = (sin_p * fine_t[0] + cos_p * fine_t[1]).astype(jnp.bfloat16)
        return carry

    lax.fori_loop(0, K // 16, rows_t, 0, unroll=2)


def spectral(rows, points, damp_rows, packed, table, table_t, twiddle, raw, spread, result):
    scale = 2.0 / jnp.full((rows, KT), points, jnp.float32)

    def tile(t, carry):
        at = pl.multiple_of(t * KT, KT)
        cos_at, sin_at = pl.ds(at, KT), pl.ds(K + at, KT)
        raw[0] = jnp.dot(packed[...], table[:, cos_at], preferred_element_type=jnp.float32)
        raw[1] = jnp.dot(packed[...], table[:, sin_at], preferred_element_type=jnp.float32)
        sum_c = jnp.zeros((rows, KT), jnp.float32)
        sum_s = jnp.zeros((rows, KT), jnp.float32)
        for l in range(NBLK):
            part_c, part_s = raw[0, l * rows : (l + 1) * rows, :], raw[1, l * rows : (l + 1) * rows, :]
            tw_c, tw_s = twiddle[0, l : l + 1, cos_at], twiddle[1, l : l + 1, cos_at]
            sum_c += tw_c * part_c - tw_s * part_s
            sum_s += tw_s * part_c + tw_c * part_s
        ratio = (iota((rows, KT), 1) + (t * KT).astype(jnp.float32)) * (1.0 / K)
        damping = scale / (1.0 + damp_rows * ratio * ratio)
        sum_c *= damping
        sum_s *= damping
        for l in range(NBLK):
            tw_c, tw_s = twiddle[0, l : l + 1, cos_at], twiddle[1, l : l + 1, cos_at]
            spread[0, l * rows : (l + 1) * rows, :] = (tw_c * sum_c + tw_s * sum_s).astype(jnp.bfloat16)
            spread[1, l * rows : (l + 1) * rows, :] = (tw_c * sum_s - tw_s * sum_c).astype(jnp.bfloat16)
        k_rows = pl.ds(at, KT)
        add = jnp.dot(spread[0], table_t[0, k_rows, :], preferred_element_type=jnp.float32)
        add += jnp.dot(spread[1], table_t[1, k_rows, :], preferred_element_type=jnp.float32)

        @pl.when(t == 0)
        def _():
            result[...] = add

        @pl.when(t > 0)
        def _():
            result[...] += add

        return carry

    lax.fori_loop(0, K // KT, tile, 0)


def shift_rows(cells, down, edge):
    row = lax.broadcasted_iota(jnp.int32, cells.shape, 0)
    last = cells.shape[0] - 1
    if down:
        return jnp.where(row == 0, edge, pltpu.roll(cells, 1, 0))
    return jnp.where(row == last, edge, pltpu.roll(cells, last, 0))


def shift_cols(cells, right, edge):
    lane = lax.broadcasted_iota(jnp.int32, cells.shape, 1)
    last = cells.shape[1] - 1
    if right:
        return jnp.where(lane == 0, edge, pltpu.roll(cells, 1, 1))
    return jnp.where(lane == last, edge, pltpu.roll(cells, last, 1))


def window_kernel(
    n_ref, nu_ref, src_ref, dst_ref, live_ref, force_hbm, mix_hbm, mask_hbm, weight_hbm, u_hbm, v_hbm,
    out_ocean, out_u, out_v,
    force, mix, mask, weight, last_u, load_sem,
    cells, ratio, ocean, send_n, send_s, send_w, send_e, got_n, got_s, got_w, got_e, halo_send, halo_recv,
    flux, note, notes, note_send, note_recv,
    stage, got_u, got_v, fwd_send, fwd_recv,
    coarse, fine, coarse_t, fine_t, table, table_t, twiddle,
    packed, raw, spread, result, back_u, back_v, blank, back_send, back_recv, ocean_sem,
):
    me, oc = lax.axis_index("lon"), lax.axis_index("ocn")
    n_lon, n_ocn = lax.axis_size("lon"), lax.axis_size("ocn")
    levels = cells.shape[0] - 1
    last_owner = n_lon - 1
    share = 2
    source = me < NBLK

    def mine(t):
        return pl.ds(share * t, share)

    loads = [
        pltpu.make_async_copy(force_hbm, force, load_sem.at[0]),
        pltpu.make_async_copy(mix_hbm, mix, load_sem.at[1]),
        pltpu.make_async_copy(mask_hbm, mask, load_sem.at[2]),
        pltpu.make_async_copy(weight_hbm.at[pl.ds(0, NBLK)], weight, load_sem.at[3]),
        pltpu.make_async_copy(u_hbm.at[mine(last_owner)], last_u, load_sem.at[4]),
    ]
    for load in loads:
        load.start()

    barrier = pltpu.get_barrier_semaphore()

    def greet(i, carry):
        pl.semaphore_signal(barrier, inc=1, device_id={"lon": lax.rem(me + i, n_lon)}, device_id_type=MESH)
        return carry

    lax.fori_loop(1, n_lon, greet, 0)

    @pl.when(oc > 0)
    def _():
        pl.semaphore_signal(barrier, inc=1, device_id={"ocn": oc - 1}, device_id_type=MESH)

    @pl.when(oc < n_ocn - 1)
    def _():
        pl.semaphore_signal(barrier, inc=1, device_id={"ocn": oc + 1}, device_id_type=MESH)

    for load in loads[:3]:
        load.wait()
    zero = jnp.zeros(force.shape[1:], jnp.float32)
    rat, val, below = zero, zero, zero
    for z in range(levels - 1, -1, -1):
        above = mix[z - 1] if z > 0 else zero
        inv = 1.0 / (1.0 + above + below * (1.0 - rat))
        val = (force[z] + below * val) * inv
        rat = above * inv
        cells[z] = val
        ratio[z] = rat
        below = above
    lane = lax.broadcasted_iota(jnp.int32, zero.shape, 1)
    west, east = zero, zero
    send_n[pl.ds(levels, 8), :] = zero
    send_s[pl.ds(levels, 8), :] = zero
    s = zero
    for z in range(levels + 1):
        if z < levels:
            s = cells[z] + ratio[z] * s if z > 0 else cells[0]
        else:
            s = mask[...].astype(jnp.float32)
        cells[z] = s
        send_n[z : z + 1, :] = s[0:1, :]
        send_s[z : z + 1, :] = s[7:8, :]
        west = jnp.where(lane == z, jnp.broadcast_to(s[:, 0:1], s.shape), west)
        east = jnp.where(lane == z, jnp.broadcast_to(s[:, BLK - 1 : BLK], s.shape), east)
    send_w[...] = west
    send_e[...] = east

    pl.semaphore_wait(barrier, n_lon - 1 + (oc > 0).astype(jnp.int32) + (oc < n_ocn - 1).astype(jnp.int32))

    sides = (
        (oc > 0, oc < n_ocn - 1, {"ocn": oc - 1}, send_n, got_s),
        (oc < n_ocn - 1, oc > 0, {"ocn": oc + 1}, send_s, got_n),
        (me > 0, me < n_lon - 1, {"lon": me - 1}, send_w, got_e),
        (me < n_lon - 1, me > 0, {"lon": me + 1}, send_e, got_w),
    )

    def halo(i):
        has, gets, where, out, into = sides[i]
        return has, gets, into, pltpu.make_async_remote_copy(
            src_ref=out, dst_ref=into, send_sem=halo_send.at[i], recv_sem=halo_recv.at[i], device_id=where, device_id_type=MESH
        )

    for i in range(4):
        has, gets, into, copy = halo(i)
        pl.when(has)(copy.start)

        @pl.when(jnp.logical_not(gets))
        def _(into=into):
            into[...] = jnp.zeros_like(into)

    def forward(i, carry):
        t = lax.rem(me + i, n_lon)
        pltpu.make_async_remote_copy(
            src_ref=v_hbm.at[mine(t)], dst_ref=got_v.at[me], send_sem=fwd_send.at[0], recv_sem=fwd_recv.at[0], device_id={"lon": t}, device_id_type=MESH
        ).start()

        @pl.when(t != last_owner)
        def _():
            pltpu.make_async_remote_copy(
                src_ref=u_hbm.at[mine(t)], dst_ref=got_u.at[me], send_sem=fwd_send.at[1], recv_sem=fwd_recv.at[1], device_id={"lon": t}, device_id_type=MESH
            ).start()

        return carry

    @pl.when(source)
    def _():
        lax.fori_loop(1, n_lon, forward, 0)
        pltpu.make_async_copy(v_hbm.at[mine(me)], got_v.at[me], fwd_recv.at[0]).start()
        pltpu.make_async_copy(u_hbm.at[mine(me)], got_u.at[me], fwd_recv.at[1]).start()

    points = n_ref[0].astype(jnp.float32)
    build_tables(points, coarse, fine, coarse_t, fine_t, table, table_t, twiddle)

    for i in range(4):
        has, gets, into, copy = halo(i)
        pl.when(gets)(copy.wait_recv)
        pl.when(has)(copy.wait_send)

    m = cells[levels]
    m_n, m_s = shift_rows(m, True, got_n[levels : levels + 1, :]), shift_rows(m, False, got_s[levels : levels + 1, :])
    m_w = shift_cols(m, True, jnp.broadcast_to(got_w[:, levels : levels + 1], m.shape))
    m_e = shift_cols(m, False, jnp.broadcast_to(got_e[:, levels : levels + 1], m.shape))

    def mixed(z):
        s = cells[z]
        near = m_n * (shift_rows(s, True, got_n[z : z + 1, :]) - s)
        near += m_s * (shift_rows(s, False, got_s[z : z + 1, :]) - s)
        near += m_w * (shift_cols(s, True, jnp.broadcast_to(got_w[:, z : z + 1], s.shape)) - s)
        near += m_e * (shift_cols(s, False, jnp.broadcast_to(got_e[:, z : z + 1], s.shape)) - s)
        return m * (s + NU_MIX * near)

    surface = mixed(0)
    ocean[0] = surface
    flux[...] = surface.astype(jnp.bfloat16).astype(jnp.float32)
    loads[3].wait()

    def owner(p, carry):
        one = flux[pl.ds(src_ref[p, 0], 1), :]
        two = flux[pl.ds(src_ref[p, 1], 1), :]
        row = lax.broadcasted_iota(jnp.int32, (8, BLK), 0)
        lhs = jnp.concatenate([jnp.where(row == 0, one, 0.0), jnp.where(row == 1, two, 0.0)], 1).astype(jnp.bfloat16)
        both = jnp.concatenate([weight[p, 0], weight[p, 1]], 1)
        got = lax.dot_general(lhs, both, (((1,), (1,)), ((), ())), preferred_element_type=jnp.float32)
        code_0 = live_ref[p, 0] * (dst_ref[p, 0] + 1) - 1
        code_1 = live_ref[p, 1] * (dst_ref[p, 1] + 1) - 1
        codes = jnp.where(row == 2, code_0, code_1).astype(jnp.float32)
        note[p] = jnp.where(row < 2, got, codes)[0:4]
        return carry

    lax.fori_loop(0, NBLK, owner, 0, unroll=3)

    def tell(p, carry):
        @pl.when(p != me)
        def _():
            pltpu.make_async_remote_copy(
                src_ref=note.at[p], dst_ref=notes.at[me], send_sem=note_send, recv_sem=note_recv, device_id={"lon": p}, device_id_type=MESH
            ).start()

        return carry

    lax.fori_loop(0, NBLK, tell, 0)

    @pl.when(source)
    def _():
        pltpu.make_async_copy(note.at[me], notes.at[me], note_recv).start()

    for z in range(1, levels):
        ocean[z] = mixed(z)
    ocean_copy = pltpu.make_async_copy(ocean, out_ocean, ocean_sem)
    ocean_copy.start()
    loads[4].wait()

    @pl.when(source)
    def _():
        pltpu.make_async_copy(notes, notes, note_recv).wait()
        even = 2.0 * iota((8, BLK), 0)
        odd = even + 1.0

        def add(l, sums):
            sum_even, sum_odd = sums
            block = notes[l]
            for c in range(2):
                value, code = block[c : c + 1, :], block[c + 2 : c + 3, :]
                sum_even += jnp.where(code == even, value, 0.0)
                sum_odd += jnp.where(code == odd, value, 0.0)
            return sum_even, sum_odd

        blank_sum = jnp.zeros((8, BLK), jnp.float32)
        sum_even, sum_odd = lax.fori_loop(0, n_lon, add, (blank_sum, blank_sum), unroll=4)
        coupling = jnp.concatenate([sum_even, sum_odd], 1)
        stage[0] = last_u[0]
        stage[1] = (last_u[1].astype(jnp.float32) + coupling).astype(jnp.bfloat16)
        pltpu.make_async_remote_copy(
            src_ref=stage, dst_ref=got_u.at[me], send_sem=fwd_send.at[1], recv_sem=fwd_recv.at[1], device_id={"lon": last_owner}, device_id_type=MESH
        ).start()

    column = iota((16, SEGLON), 1)
    row = iota((16, KT), 0)
    nu = jnp.where(row < 8, nu_ref[share * me], nu_ref[share * me + 1])
    for f, (got, back, out) in enumerate(((got_v, back_v, out_v), (got_u, back_u, out_u))):
        pltpu.make_async_copy(got, got, fwd_recv.at[f]).wait()

        def pack(l, carry, got=got):
            inside = column + (l * SEGLON).astype(jnp.float32) < points
            block = got[l].astype(jnp.float32).reshape(16, SEGLON)
            packed[pl.ds(pl.multiple_of(16 * l, 16), 16), :] = jnp.where(inside, block, 0.0).astype(jnp.bfloat16)
            return carry

        lax.fori_loop(0, NBLK, pack, 0)
        spectral(16, points, nu, packed, table, table_t, twiddle, raw, spread, result)

        def unpack(l, carry, back=back, out=out, f=f):
            inside = column + (l * SEGLON).astype(jnp.float32) < points
            block = result[pl.ds(pl.multiple_of(16 * l, 16), 16), :]
            back[l] = jnp.where(inside, block, 0.0).reshape(2, 8, SEGLON).astype(jnp.bfloat16)

            @pl.when(l != me)
            def _():
                pltpu.make_async_remote_copy(
                    src_ref=back.at[l], dst_ref=out.at[mine(me)], send_sem=back_send.at[f], recv_sem=back_recv.at[f], device_id={"lon": l}, device_id_type=MESH
                ).start()

            return carry

        lax.fori_loop(0, NBLK, unpack, 0)

        @pl.when(source)
        def _(back=back, out=out, f=f):
            pltpu.make_async_copy(back.at[me], out.at[mine(me)], back_recv.at[f]).start()

        @pl.when(jnp.logical_not(source))
        def _(back=back, out=out, f=f):
            if f == 0:
                blank[...] = jnp.zeros_like(blank)
            pltpu.make_async_copy(blank, out, back_recv.at[f]).start()

    ocean_copy.wait()

    @pl.when(source)
    def _():
        for f in range(2):
            sent = v_hbm.at[pl.ds(0, share * (n_lon - 1))]
            pltpu.make_async_copy(sent, sent, fwd_send.at[f]).wait()
        told = note.at[pl.ds(0, NBLK - 1)]
        pltpu.make_async_copy(told, told, note_send).wait()

    @pl.when(jnp.logical_not(source))
    def _():
        pltpu.make_async_copy(note, note, note_send).wait()

    for f, (back, out) in enumerate(((back_v, out_v), (back_u, out_u))):

        @pl.when(source)
        def _(back=back, f=f):
            sent = back.at[pl.ds(0, NBLK - 1)]
            pltpu.make_async_copy(sent, sent, back_send.at[f]).wait()

        @pl.when(jnp.logical_not(source))
        def _(back=back, f=f):
            pltpu.make_async_copy(back, back, back_send.at[f]).wait()

        pltpu.make_async_copy(out, out, back_recv.at[f]).wait()


def per_device(
    ocean_adjoint,
    mixing_coef,
    land_mask,
    remap_src,
    remap_dst,
    remap_live,
    remap_weight,
    atm_u,
    atm_v,
    spectral_nu,
    band_points,
):
    lon_devices = lax.axis_size("lon")
    levels = ocean_adjoint.shape[0]
    slots = remap_src.shape[2:]
    tile = ocean_adjoint.shape[1:]
    m = 16 * NBLK
    f32, bf16, dma = jnp.float32, jnp.bfloat16, pltpu.SemaphoreType.DMA
    smem = pl.BlockSpec(memory_space=pltpu.SMEM)
    hbm = pl.BlockSpec(memory_space=pl.ANY)
    two = (2,) + atm_u.shape[1:]
    edge = (levels + 8, BLK)
    return pl.pallas_call(
        window_kernel,
        out_shape=(
            jax.ShapeDtypeStruct(ocean_adjoint.shape, f32),
            jax.ShapeDtypeStruct(atm_u.shape, bf16),
            jax.ShapeDtypeStruct(atm_v.shape, bf16),
        ),
        in_specs=[smem] * 5 + [hbm] * 6,
        out_specs=(hbm, hbm, hbm),
        scratch_shapes=[
            pltpu.VMEM(ocean_adjoint.shape, f32),
            pltpu.VMEM(mixing_coef.shape, f32),
            pltpu.VMEM(land_mask.shape, jnp.int32),
            pltpu.VMEM((NBLK, slots[1], BLK, BLK), bf16),
            pltpu.VMEM(two, bf16),
            dma((5,)),
            pltpu.VMEM((levels + 1,) + tile, f32),
            pltpu.VMEM((levels,) + tile, f32),
            pltpu.VMEM((levels,) + tile, f32),
            pltpu.VMEM(edge, f32),
            pltpu.VMEM(edge, f32),
            pltpu.VMEM(tile, f32),
            pltpu.VMEM(tile, f32),
            pltpu.VMEM(edge, f32),
            pltpu.VMEM(edge, f32),
            pltpu.VMEM(tile, f32),
            pltpu.VMEM(tile, f32),
            dma((4,)),
            dma((4,)),
            pltpu.VMEM(tile, f32),
            pltpu.VMEM((NBLK, 4, BLK), f32),
            pltpu.VMEM((lon_devices, 4, BLK), f32),
            dma,
            dma,
            pltpu.VMEM(two, bf16),
            pltpu.VMEM((NBLK,) + two, bf16),
            pltpu.VMEM((NBLK,) + two, bf16),
            dma((2,)),
            dma((2,)),
            pltpu.VMEM((2, 16, K), f32),
            pltpu.VMEM((2, 16, K), f32),
            pltpu.VMEM((2, K // 16, SEGLON), f32),
            pltpu.VMEM((2, 16, SEGLON), f32),
            pltpu.VMEM((SEGLON, 2 * K), bf16),
            pltpu.VMEM((2, K, SEGLON), bf16),
            pltpu.VMEM((2, TWROWS, K), f32),
            pltpu.VMEM((m, SEGLON), bf16),
            pltpu.VMEM((2, m, KT), f32),
            pltpu.VMEM((2, m, KT), bf16),
            pltpu.VMEM((m, SEGLON), f32),
            pltpu.VMEM((NBLK,) + two, bf16),
            pltpu.VMEM((NBLK,) + two, bf16),
            pltpu.VMEM(atm_u.shape, bf16),
            dma((2,)),
            dma((2,)),
            dma,
        ],
        compiler_params=pltpu.CompilerParams(collective_id=0, has_side_effects=True, vmem_limit_bytes=48 << 20),
        name="window",
    )(
        band_points,
        spectral_nu,
        remap_src.reshape(slots),
        remap_dst.reshape(slots),
        remap_live.reshape(slots),
        ocean_adjoint,
        mixing_coef,
        land_mask,
        remap_weight.reshape(remap_weight.shape[2:]),
        atm_u,
        atm_v,
    )


def solution(mesh):
    placed = (
        P(None, "ocn", "lon"),
        P(None, "ocn", "lon"),
        P("ocn", "lon"),
        P("ocn", "lon", None, None),
        P("ocn", "lon", None, None),
        P("ocn", "lon", None, None),
        P("ocn", "lon", None, None, None, None),
        P(None, "ocn", "lon"),
        P(None, "ocn", "lon"),
        P(),
        P("ocn"),
    )
    return jax.shard_map(
        per_device,
        mesh=mesh,
        in_specs=placed,
        out_specs=(P(None, "ocn", "lon"), P(None, "ocn", "lon"), P(None, "ocn", "lon")),
        check_vma=False,
    )
```

time: 113 us -> 43.9 us (0.39)
  waiting for transfers between devices: 41.2 us -> 0 us
  starting transfers between devices: 33.5 us -> 0 us
  Pallas kernels: 15.9 us -> 31.2 us
  blocking collectives: 12.4 us -> 0 us
  local copies, waits for them, and re-layouts: 2.31 us -> 11 us
  other arithmetic: 5.36 us -> 0 us
    all_to_all x4 -> x0, waiting for transfers between devices: 32.7 us -> none  [per_device(): lax.all_to_all(x, 'lon', split_axis=0, concat_axis=0, tiled=True)]
    all_to_all x4 -> x0, starting transfers between devices: 19.7 us -> none  [per_device(): lax.all_to_all(x, 'lon', split_axis=0, concat_axis=0, tiled=True)]
    pallas_call x3 -> x1, Pallas kernels: 15.9 us -> 31.2 us  [per_device(): pl.pallas_call(window_kernel, out_shape=(jax.ShapeDtypeStruct(ocean_adjoi...]
    ppermute x4 -> x0, starting transfers between devices: 13.8 us -> none  [the longest x2 9.95 us: with_halo(): lax.ppermute(tail, axis, [(i, (i + 1) % count) for i in range(ends)])]
    all_to_all x1 -> x0, blocking collectives: 12.4 us -> none  [per_device(): lax.all_to_all(x, 'lon', split_axis=0, concat_axis=0, tiled=True)]
    ppermute x4 -> x0, waiting for transfers between devices: 8.48 us -> none  [the longest x2 8.16 us: with_halo(): lax.ppermute(head, axis, [((i + 1) % count, i) for i in range(ends)])]
    unnamed x15 -> x17, local copies, waits for them, and re-layouts: 1.52 us -> 8.7 us
    concatenate x3 -> x0, other arithmetic: 2.35 us -> none  [the longest x1 0.96 us: with_halo(): jnp.concatenate([lax.ppermute(tail, axis, [(i, (i + 1) % count) for i in...]
  transfers between devices with their start and end apart: 8 -> 0, of which waited for: 7 -> 0; matrix products, arithmetic and copies ran while one was open for 2% -> 0% of each run, Pallas kernels for 0% -> 0%
where the time goes in v2:
time: 43.9 us; the launch traced here: 43.5 us
  Pallas kernels  31.2 us (71%)
  local copies, waits for them, and re-layouts  11 us (25%)
  between operations  1.3 us (3%)
    pallas_call x1, Pallas kernels, per_device(): pl.pallas_call(window_kernel, out_shape=(jax.ShapeDtypeStruct(ocean_adjoi...  31.2 us
    unnamed x17, local copies, waits for them, and re-layouts  8.7 us

profile of v2, /device:TPU:97, one launch (start us, length us, event | category | flops | bytes accessed | tf_op | source)
XLA Modules:
  0.0 43.5 jit_solution(8630804568411267290)
XLA Ops:
  1.3 0.8 %copy.14.src_ref = s32[32,2]{1,0:T(8,128)S(1)} copy(s32[32,2]{0,1:T(2,128)} %bitcast.5) | data formatting | bytes 512 | tf_op jit(solution)/shard_map/reshape | solution.py:485
  2.0 0.8 %copy.15.dst_ref = s32[32,2]{1,0:T(8,128)S(1)} copy(s32[32,2]{0,1:T(2,128)} %bitcast.6) | data formatting | bytes 512 | tf_op jit(solution)/shard_map/reshape | solution.py:486
  2.8 0.8 %copy.16.live_ref = s32[32,2]{1,0:T(8,128)S(1)} copy(s32[32,2]{0,1:T(2,128)} %bitcast.7) | data formatting | bytes 512 | tf_op jit(solution)/shard_map/reshape | solution.py:487
  3.6 0.0 copy-start
  3.6 1.6 %copy-done = bf16[1,1,32,2,128,128]{5,4,3,2,1,0:T(8,128)(2,1)S(1)} copy-done((bf16[1,1,32,2,128,128]{5,4,3,2,1,0:T(8,128)(2,1)S(1)}, bf16[1,1,32,2,128,128]{5,4,3,2,1,0:T(8,128)(2,1)}, u32[]{:S(2)}) %copy-start) | copy-done | bytes 2097176
  5.1 0.0 copy-start.1
  5.2 0.9 %copy-done.1 = bf16[64,8,256]{2,1,0:T(8,128)(2,1)S(1)} copy-done((bf16[64,8,256]{2,1,0:T(8,128)(2,1)S(1)}, bf16[64,8,256]{2,1,0:T(8,128)(2,1)}, u32[]{:S(2)}) %copy-start.1) | copy-done | bytes 262168
  6.1 0.0 copy-start.2
  6.1 0.9 %copy-done.2 = bf16[64,8,256]{2,1,0:T(8,128)(2,1)S(1)} copy-done((bf16[64,8,256]{2,1,0:T(8,128)(2,1)S(1)}, bf16[64,8,256]{2,1,0:T(8,128)(2,1)}, u32[]{:S(2)}) %copy-start.2) | copy-done | bytes 262168
  7.0 0.0 copy-start.3
  7.1 0.9 %copy-done.3 = f32[32,8,128]{2,1,0:T(8,128)S(1)} copy-done((f32[32,8,128]{2,1,0:T(8,128)S(1)}, f32[32,8,128]{2,1,0:T(8,128)}, u32[]{:S(2)}) %copy-start.3) | copy-done | bytes 131096
  8.0 0.0 copy-start.4
  8.0 0.9 %copy-done.4 = f32[31,8,128]{2,1,0:T(8,128)S(1)} copy-done((f32[31,8,128]{2,1,0:T(8,128)S(1)}, f32[31,8,128]{2,1,0:T(8,128)}, u32[]{:S(2)}) %copy-start.4) | copy-done | bytes 127000
  8.9 0.0 copy-start.5
  8.9 0.7 %copy-done.5 = s32[8,128]{1,0:T(8,128)S(1)} copy-done((s32[8,128]{1,0:T(8,128)S(1)}, s32[8,128]{1,0:T(8,128)}, u32[]{:S(2)}) %copy-start.5) | copy-done | bytes 4120
  9.5 0.0 copy-start.6
  9.5 0.7 %copy-done.6 = f32[64]{0:T(128)S(1)} copy-done((f32[64]{0:T(128)S(1)}, f32[64]{0:T(128)}, u32[]{:S(2)}) %copy-start.6) | copy-done | bytes 280
  10.2 31.2 %window.1 = (f32[32,8,128]{2,1,0:T(8,128)S(1)}, bf16[64,8,256]{2,1,0:T(8,128)(2,1)S(1)}, bf16[64,8,256]{2,1,0:T(8,128)(2,1)S(1)}) custom-call(s32[1]{0:T(128)S(6)} %copy.20.n_ref, f32[64]{0:T(128)S(1)} %copy-done.6, s32[32,2]{1,0:T(8,128)S(1)} %copy.14.src_ref, s32[32,2]{1,0:T(8,128)S(1)} %copy.15.dst_ref, s32[32,2]{1,0:T(8,128)S(1)} %copy.16.live_ref, ...), custom_call_target="tpu_custom_call" | custom-call | tf_op jit(solution)/shard_map/window/pallas_call | solution.py:423
  41.4 0.7 %copy.21 = f32[32,8,128]{2,1,0:T(8,128)} copy(f32[32,8,128]{2,1,0:T(8,128)S(1)} %get-tuple-element.6) | data formatting | bytes 262144
  42.1 0.7 %copy.22 = bf16[64,8,256]{2,1,0:T(8,128)(2,1)} copy(bf16[64,8,256]{2,1,0:T(8,128)(2,1)S(1)} %get-tuple-element.7) | data formatting | bytes 524288
  42.8 0.7 %copy.23 = bf16[64,8,256]{2,1,0:T(8,128)(2,1)} copy(bf16[64,8,256]{2,1,0:T(8,128)(2,1)S(1)} %get-tuple-element.8) | data formatting | bytes 524288
Async XLA Ops:
  3.6 1.6 %copy-start = (bf16[1,1,32,2,128,128]{5,4,3,2,1,0:T(8,128)(2,1)S(1)}, bf16[1,1,32,2,128,128]{5,4,3,2,1,0:T(8,128)(2,1)}, u32[]{:S(2)}) copy-start(bf16[1,1,32,2,128,128]{5,4,3,2,1,0:T(8,128)(2,1)} %param.17) | copy-start | bytes 6291460
  5.1 0.9 %copy-start.1 = (bf16[64,8,256]{2,1,0:T(8,128)(2,1)S(1)}, bf16[64,8,256]{2,1,0:T(8,128)(2,1)}, u32[]{:S(2)}) copy-start(bf16[64,8,256]{2,1,0:T(8,128)(2,1)} %u_hbm.1) | copy-start | bytes 786436
  6.1 0.9 %copy-start.2 = (bf16[64,8,256]{2,1,0:T(8,128)(2,1)S(1)}, bf16[64,8,256]{2,1,0:T(8,128)(2,1)}, u32[]{:S(2)}) copy-start(bf16[64,8,256]{2,1,0:T(8,128)(2,1)} %v_hbm.1) | copy-start | bytes 786436
  7.0 0.9 %copy-start.3 = (f32[32,8,128]{2,1,0:T(8,128)S(1)}, f32[32,8,128]{2,1,0:T(8,128)}, u32[]{:S(2)}) copy-start(f32[32,8,128]{2,1,0:T(8,128)} %force_hbm.1) | copy-start | bytes 393220
  8.0 0.9 %copy-start.4 = (f32[31,8,128]{2,1,0:T(8,128)S(1)}, f32[31,8,128]{2,1,0:T(8,128)}, u32[]{:S(2)}) copy-start(f32[31,8,128]{2,1,0:T(8,128)} %mix_hbm.1) | copy-start | bytes 380932
  8.9 0.7 %copy-start.5 = (s32[8,128]{1,0:T(8,128)S(1)}, s32[8,128]{1,0:T(8,128)}, u32[]{:S(2)}) copy-start(s32[8,128]{1,0:T(8,128)} %mask_hbm.1) | copy-start | bytes 12292
  9.5 0.7 %copy-start.6 = (f32[64]{0:T(128)S(1)}, f32[64]{0:T(128)}, u32[]{:S(2)}) copy-start(f32[64]{0:T(128)} %nu_ref.1) | copy-start | bytes 772

commit v3 on v2

--- a/solution.py
+++ b/solution.py
@@ -61,51 +61,50 @@
     def rows_t(p, carry):
         cos_p, sin_p = coarse_t[0, pl.ds(p, 1), :], coarse_t[1, pl.ds(p, 1), :]
         here = pl.ds(pl.multiple_of(16 * p, 16), 16)
-        table_t[0, here, :] = (cos_p * fine_t[0] - sin_p * fine_t[1]).astype(jnp.bfloat16)
-        table_t[1, here, :] = (sin_p * fine_t[0] + cos_p * fine_t[1]).astype(jnp.bfloat16)
+        table_t[here, :] = (cos_p * fine_t[0] - sin_p * fine_t[1]).astype(jnp.bfloat16)
+        table_t[pl.ds(pl.multiple_of(K + 16 * p, 16), 16), :] = (sin_p * fine_t[0] + cos_p * fine_t[1]).astype(jnp.bfloat16)
         return carry
 
     lax.fori_loop(0, K // 16, rows_t, 0, unroll=2)
 
 
-def spectral(rows, points, damp_rows, packed, table, table_t, twiddle, raw, spread, result):
+def spectral(rows, points, viscosity, packed, table, table_t, twiddle, raw, spread, result):
+    total = NBLK * rows
+    half = (total // 2 + 15) // 16 * 16
     scale = 2.0 / jnp.full((rows, KT), points, jnp.float32)
 
-    def tile(t, carry):
-        at = pl.multiple_of(t * KT, KT)
-        cos_at, sin_at = pl.ds(at, KT), pl.ds(K + at, KT)
-        raw[0] = jnp.dot(packed[...], table[:, cos_at], preferred_element_type=jnp.float32)
-        raw[1] = jnp.dot(packed[...], table[:, sin_at], preferred_element_type=jnp.float32)
+    def transform(t):
+        for part in range(2):
+            at = part * K + t * KT
+            raw[t, part] = jnp.dot(packed[...], table[:, at : at + KT], preferred_element_type=jnp.float32)
+
+    def twist(t):
+        cos_at, sin_at = slice(t * KT, (t + 1) * KT), slice(K + t * KT, K + (t + 1) * KT)
         sum_c = jnp.zeros((rows, KT), jnp.float32)
         sum_s = jnp.zeros((rows, KT), jnp.float32)
         for l in range(NBLK):
-            part_c, part_s = raw[0, l * rows : (l + 1) * rows, :], raw[1, l * rows : (l + 1) * rows, :]
+            here = slice(l * rows, (l + 1) * rows)
+            part_c, part_s = raw[t, 0, here, :], raw[t, 1, here, :]
             tw_c, tw_s = twiddle[0, l : l + 1, cos_at], twiddle[1, l : l + 1, cos_at]
             sum_c += tw_c * part_c - tw_s * part_s
             sum_s += tw_s * part_c + tw_c * part_s
-        ratio = (iota((rows, KT), 1) + (t * KT).astype(jnp.float32)) * (1.0 / K)
-        damping = scale / (1.0 + damp_rows * ratio * ratio)
+        ratio = (iota((rows, KT), 1) + float(t * KT)) * (1.0 / K)
+        damping = scale / (1.0 + viscosity * ratio * ratio)
         sum_c *= damping
         sum_s *= damping
         for l in range(NBLK):
+            here = slice(l * rows, (l + 1) * rows)
             tw_c, tw_s = twiddle[0, l : l + 1, cos_at], twiddle[1, l : l + 1, cos_at]
-            spread[0, l * rows : (l + 1) * rows, :] = (tw_c * sum_c + tw_s * sum_s).astype(jnp.bfloat16)
-            spread[1, l * rows : (l + 1) * rows, :] = (tw_c * sum_s - tw_s * sum_c).astype(jnp.bfloat16)
-        k_rows = pl.ds(at, KT)
-        add = jnp.dot(spread[0], table_t[0, k_rows, :], preferred_element_type=jnp.float32)
-        add += jnp.dot(spread[1], table_t[1, k_rows, :], preferred_element_type=jnp.float32)
-
-        @pl.when(t == 0)
-        def _():
-            result[...] = add
-
-        @pl.when(t > 0)
-        def _():
-            result[...] += add
-
-        return carry
-
-    lax.fori_loop(0, K // KT, tile, 0)
+            spread[here, cos_at] = (tw_c * sum_c + tw_s * sum_s).astype(jnp.bfloat16)
+            spread[here, sin_at] = (tw_c * sum_s - tw_s * sum_c).astype(jnp.bfloat16)
+
+    transform(0)
+    for t in range(K // KT):
+        if t + 1 < K // KT:
+            transform(t + 1)
+        twist(t)
+    for here in (slice(0, half), slice(half, total)):
+        result[here] = jnp.dot(spread[here], table_t[...], preferred_element_type=jnp.float32)
 
 
 def shift_rows(cells, down, edge):
@@ -125,9 +124,9 @@
 
 
 def window_kernel(
-    n_ref, nu_ref, src_ref, dst_ref, live_ref, force_hbm, mix_hbm, mask_hbm, weight_hbm, u_hbm, v_hbm,
+    n_ref, nu_hbm, src_hbm, dst_hbm, live_hbm, force_hbm, mix_hbm, mask_hbm, weight_hbm, u_hbm, v_hbm,
     out_ocean, out_u, out_v,
-    force, mix, mask, weight, last_u, load_sem,
+    nu_ref, src_ref, dst_ref, live_ref, force, mix, mask, weight, last_u, load_sem,
     cells, ratio, ocean, send_n, send_s, send_w, send_e, got_n, got_s, got_w, got_e, halo_send, halo_recv,
     flux, note, notes, note_send, note_recv,
     stage, got_u, got_v, fwd_send, fwd_recv,
@@ -150,6 +149,10 @@
         pltpu.make_async_copy(mask_hbm, mask, load_sem.at[2]),
         pltpu.make_async_copy(weight_hbm.at[pl.ds(0, NBLK)], weight, load_sem.at[3]),
         pltpu.make_async_copy(u_hbm.at[mine(last_owner)], last_u, load_sem.at[4]),
+        pltpu.make_async_copy(nu_hbm, nu_ref, load_sem.at[5]),
+        pltpu.make_async_copy(src_hbm, src_ref, load_sem.at[6]),
+        pltpu.make_async_copy(dst_hbm, dst_ref, load_sem.at[7]),
+        pltpu.make_async_copy(live_hbm, live_ref, load_sem.at[8]),
     ]
     for load in loads:
         load.start()
@@ -169,6 +172,9 @@
     @pl.when(oc < n_ocn - 1)
     def _():
         pl.semaphore_signal(barrier, inc=1, device_id={"ocn": oc + 1}, device_id_type=MESH)
+
+    points = n_ref[0].astype(jnp.float32)
+    build_tables(points, coarse, fine, coarse_t, fine_t, table, table_t, twiddle)
 
     for load in loads[:3]:
         load.wait()
@@ -243,9 +249,6 @@
         pltpu.make_async_copy(v_hbm.at[mine(me)], got_v.at[me], fwd_recv.at[0]).start()
         pltpu.make_async_copy(u_hbm.at[mine(me)], got_u.at[me], fwd_recv.at[1]).start()
 
-    points = n_ref[0].astype(jnp.float32)
-    build_tables(points, coarse, fine, coarse_t, fine_t, table, table_t, twiddle)
-
     for i in range(4):
         has, gets, into, copy = halo(i)
         pl.when(gets)(copy.wait_recv)
@@ -267,17 +270,18 @@
     surface = mixed(0)
     ocean[0] = surface
     flux[...] = surface.astype(jnp.bfloat16).astype(jnp.float32)
-    loads[3].wait()
+    for load in loads[3:4] + loads[6:]:
+        load.wait()
 
     def owner(p, carry):
-        one = flux[pl.ds(src_ref[p, 0], 1), :]
-        two = flux[pl.ds(src_ref[p, 1], 1), :]
+        one = flux[pl.ds(src_ref[0, p], 1), :]
+        two = flux[pl.ds(src_ref[1, p], 1), :]
         row = lax.broadcasted_iota(jnp.int32, (8, BLK), 0)
         lhs = jnp.concatenate([jnp.where(row == 0, one, 0.0), jnp.where(row == 1, two, 0.0)], 1).astype(jnp.bfloat16)
         both = jnp.concatenate([weight[p, 0], weight[p, 1]], 1)
         got = lax.dot_general(lhs, both, (((1,), (1,)), ((), ())), preferred_element_type=jnp.float32)
-        code_0 = live_ref[p, 0] * (dst_ref[p, 0] + 1) - 1
-        code_1 = live_ref[p, 1] * (dst_ref[p, 1] + 1) - 1
+        code_0 = live_ref[0, p] * (dst_ref[0, p] + 1) - 1
+        code_1 = live_ref[1, p] * (dst_ref[1, p] + 1) - 1
         codes = jnp.where(row == 2, code_0, code_1).astype(jnp.float32)
         note[p] = jnp.where(row < 2, got, codes)[0:4]
         return carry
@@ -329,6 +333,7 @@
             src_ref=stage, dst_ref=got_u.at[me], send_sem=fwd_send.at[1], recv_sem=fwd_recv.at[1], device_id={"lon": last_owner}, device_id_type=MESH
         ).start()
 
+    loads[5].wait()
     column = iota((16, SEGLON), 1)
     row = iota((16, KT), 0)
     nu = jnp.where(row < 8, nu_ref[share * me], nu_ref[share * me + 1])
@@ -395,6 +400,15 @@
             pltpu.make_async_copy(back, back, back_send.at[f]).wait()
 
         pltpu.make_async_copy(out, out, back_recv.at[f]).wait()
+
+
+def finish_kernel(ocean_in, u_in, v_in, ocean_out, u_out, v_out, sems):
+    pairs = ((ocean_in, ocean_out), (u_in, u_out), (v_in, v_out))
+    copies = [pltpu.make_async_copy(here, there, sems.at[i]) for i, (here, there) in enumerate(pairs)]
+    for copy in copies:
+        copy.start()
+    for copy in copies:
+        copy.wait()
 
 
 def per_device(
@@ -417,25 +431,31 @@
     m = 16 * NBLK
     f32, bf16, dma = jnp.float32, jnp.bfloat16, pltpu.SemaphoreType.DMA
     smem = pl.BlockSpec(memory_space=pltpu.SMEM)
-    hbm = pl.BlockSpec(memory_space=pl.ANY)
+    hbm = pl.BlockSpec(memory_space=pltpu.HBM)
+    anywhere = pl.BlockSpec(memory_space=pl.ANY)
     two = (2,) + atm_u.shape[1:]
     edge = (levels + 8, BLK)
-    return pl.pallas_call(
+    shapes = (
+        jax.ShapeDtypeStruct(ocean_adjoint.shape, f32),
+        jax.ShapeDtypeStruct(atm_u.shape, bf16),
+        jax.ShapeDtypeStruct(atm_v.shape, bf16),
+    )
+    results = pl.pallas_call(
         window_kernel,
-        out_shape=(
-            jax.ShapeDtypeStruct(ocean_adjoint.shape, f32),
-            jax.ShapeDtypeStruct(atm_u.shape, bf16),
-            jax.ShapeDtypeStruct(atm_v.shape, bf16),
-        ),
-        in_specs=[smem] * 5 + [hbm] * 6,
-        out_specs=(hbm, hbm, hbm),
+        out_shape=shapes,
+        in_specs=[smem] + [hbm] * 10,
+        out_specs=(anywhere, anywhere, anywhere),
         scratch_shapes=[
+            pltpu.SMEM(spectral_nu.shape, f32),
+            pltpu.SMEM(slots[::-1], jnp.int32),
+            pltpu.SMEM(slots[::-1], jnp.int32),
+            pltpu.SMEM(slots[::-1], jnp.int32),
             pltpu.VMEM(ocean_adjoint.shape, f32),
             pltpu.VMEM(mixing_coef.shape, f32),
             pltpu.VMEM(land_mask.shape, jnp.int32),
             pltpu.VMEM((NBLK, slots[1], BLK, BLK), bf16),
             pltpu.VMEM(two, bf16),
-            dma((5,)),
+            dma((9,)),
             pltpu.VMEM((levels + 1,) + tile, f32),
             pltpu.VMEM((levels,) + tile, f32),
             pltpu.VMEM((levels,) + tile, f32),
@@ -464,11 +484,11 @@
             pltpu.VMEM((2, K // 16, SEGLON), f32),
             pltpu.VMEM((2, 16, SEGLON), f32),
             pltpu.VMEM((SEGLON, 2 * K), bf16),
-            pltpu.VMEM((2, K, SEGLON), bf16),
+            pltpu.VMEM((2 * K, SEGLON), bf16),
             pltpu.VMEM((2, TWROWS, K), f32),
             pltpu.VMEM((m, SEGLON), bf16),
-            pltpu.VMEM((2, m, KT), f32),
-            pltpu.VMEM((2, m, KT), bf16),
+            pltpu.VMEM((K // KT, 2, m, KT), f32),
+            pltpu.VMEM((m, 2 * K), bf16),
             pltpu.VMEM((m, SEGLON), f32),
             pltpu.VMEM((NBLK,) + two, bf16),
             pltpu.VMEM((NBLK,) + two, bf16),
@@ -477,14 +497,14 @@
             dma((2,)),
             dma,
         ],
-        compiler_params=pltpu.CompilerParams(collective_id=0, has_side_effects=True, vmem_limit_bytes=48 << 20),
+        compiler_params=pltpu.CompilerParams(collective_id=0, has_side_effects=True),
         name="window",
     )(
         band_points,
         spectral_nu,
-        remap_src.reshape(slots),
-        remap_dst.reshape(slots),
-        remap_live.reshape(slots),
+        remap_src.reshape(slots).T,
+        remap_dst.reshape(slots).T,
+        remap_live.reshape(slots).T,
         ocean_adjoint,
         mixing_coef,
         land_mask,
@@ -492,6 +512,14 @@
         atm_u,
         atm_v,
     )
+    return pl.pallas_call(
+        finish_kernel,
+        out_shape=shapes,
+        in_specs=[anywhere] * 3,
+        out_specs=(hbm, hbm, hbm),
+        scratch_shapes=[dma((3,))],
+        name="finish",
+    )(*results)
 
 
 def solution(mesh):

time: 43.9 us -> 49.2 us (1.12)
  Pallas kernels: 31.2 us -> 47.2 us
  local copies, waits for them, and re-layouts: 11 us -> 0 us
    pallas_call x1 -> x2, Pallas kernels: 31.2 us -> 47.2 us  [the longest x1 26.3 us: per_device(): pl.pallas_call(window_kernel, out_shape=shapes, in_specs=[smem] + [hbm] *...]
    unnamed x17 -> x0, local copies, waits for them, and re-layouts: 8.7 us -> none
    reshape x3 -> x0, local copies, waits for them, and re-layouts: 2.28 us -> none  [the longest x1 0.76 us: per_device(): remap_src.reshape(slots)]
where the time goes in v3:
time: 49.2 us; the launch traced here: 48.5 us
  Pallas kernels  47.2 us (96%)
  between operations  1.29 us (3%)
    pallas_call x1, Pallas kernels, per_device(): pl.pallas_call(window_kernel, out_shape=shapes, in_specs=[smem] + [hbm] *...  26.3 us
    pallas_call x1, Pallas kernels, per_device(): pl.pallas_call(finish_kernel, out_shape=shapes, in_specs=[anywhere] * 3,...  21 us

profile of v3, /device:TPU:97, one launch (start us, length us, event | category | flops | bytes accessed | tf_op | source)
XLA Modules:
  0.0 48.5 jit_solution(1230346903969063314)
XLA Ops:
  1.3 26.3 %window.1 = (f32[32,8,128]{2,1,0:T(8,128)}, bf16[64,8,256]{2,1,0:T(8,128)(2,1)}, bf16[64,8,256]{2,1,0:T(8,128)(2,1)}) custom-call(s32[1]{0:T(128)S(6)} %copy.14.n_ref, f32[64]{0:T(128)} %nu_hbm.1, s32[2,32]{1,0:T(2,128)} %bitcast.11, s32[2,32]{1,0:T(2,128)} %bitcast.12, s32[2,32]{1,0:T(2,128)} %bitcast.13, f32[32,8,128]{2,1,0:T(8,128)} %force_hbm.1, ...), custom_call_target="tpu_custom_call" | custom-call | tf_op jit(solution)/shard_map/window/pallas_call | solution.py:443
  27.6 21.0 %finish.1 = (f32[32,8,128]{2,1,0:T(8,128)}, bf16[64,8,256]{2,1,0:T(8,128)(2,1)}, bf16[64,8,256]{2,1,0:T(8,128)(2,1)}) custom-call(f32[32,8,128]{2,1,0:T(8,128)} %get-tuple-element.6.ocean_in, bf16[64,8,256]{2,1,0:T(8,128)(2,1)} %get-tuple-element.7.u_in, bf16[64,8,256]{2,1,0:T(8,128)(2,1)} %get-tuple-element.8.v_in), custom_call_target="tpu_custom_call" | custom-call | tf_op jit(solution)/shard_map/finish/pallas_call | solution.py:515

commit v4 on v3

--- a/solution.py
+++ b/solution.py
@@ -172,9 +172,6 @@
     @pl.when(oc < n_ocn - 1)
     def _():
         pl.semaphore_signal(barrier, inc=1, device_id={"ocn": oc + 1}, device_id_type=MESH)
-
-    points = n_ref[0].astype(jnp.float32)
-    build_tables(points, coarse, fine, coarse_t, fine_t, table, table_t, twiddle)
 
     for load in loads[:3]:
         load.wait()
@@ -229,25 +226,30 @@
         def _(into=into):
             into[...] = jnp.zeros_like(into)
 
-    def forward(i, carry):
-        t = lax.rem(me + i, n_lon)
-        pltpu.make_async_remote_copy(
-            src_ref=v_hbm.at[mine(t)], dst_ref=got_v.at[me], send_sem=fwd_send.at[0], recv_sem=fwd_recv.at[0], device_id={"lon": t}, device_id_type=MESH
-        ).start()
-
-        @pl.when(t != last_owner)
+    def send_rows(f, field, got):
+        def forward(i, carry):
+            t = lax.rem(me + i, n_lon)
+
+            def start():
+                pltpu.make_async_remote_copy(
+                    src_ref=field.at[mine(t)], dst_ref=got.at[me], send_sem=fwd_send.at[f], recv_sem=fwd_recv.at[f], device_id={"lon": t}, device_id_type=MESH
+                ).start()
+
+            if f == 0:
+                start()
+            else:
+                pl.when(t != last_owner)(start)
+            return carry
+
+        @pl.when(source)
         def _():
-            pltpu.make_async_remote_copy(
-                src_ref=u_hbm.at[mine(t)], dst_ref=got_u.at[me], send_sem=fwd_send.at[1], recv_sem=fwd_recv.at[1], device_id={"lon": t}, device_id_type=MESH
-            ).start()
-
-        return carry
-
-    @pl.when(source)
-    def _():
-        lax.fori_loop(1, n_lon, forward, 0)
-        pltpu.make_async_copy(v_hbm.at[mine(me)], got_v.at[me], fwd_recv.at[0]).start()
-        pltpu.make_async_copy(u_hbm.at[mine(me)], got_u.at[me], fwd_recv.at[1]).start()
+            lax.fori_loop(1, n_lon, forward, 0)
+            pltpu.make_async_copy(field.at[mine(me)], got.at[me], fwd_recv.at[f]).start()
+
+    send_rows(0, v_hbm, got_v)
+
+    points = n_ref[0].astype(jnp.float32)
+    build_tables(points, coarse, fine, coarse_t, fine_t, table, table_t, twiddle)
 
     for i in range(4):
         has, gets, into, copy = halo(i)
@@ -303,6 +305,7 @@
     def _():
         pltpu.make_async_copy(note.at[me], notes.at[me], note_recv).start()
 
+    send_rows(1, u_hbm, got_u)
     for z in range(1, levels):
         ocean[z] = mixed(z)
     ocean_copy = pltpu.make_async_copy(ocean, out_ocean, ocean_sem)
@@ -442,7 +445,7 @@
     )
     results = pl.pallas_call(
         window_kernel,
-        out_shape=shapes,
+        out_shape=tuple(pltpu.VMEM(x.shape, x.dtype) for x in shapes),
         in_specs=[smem] + [hbm] * 10,
         out_specs=(anywhere, anywhere, anywhere),
         scratch_shapes=[
@@ -515,9 +518,10 @@
     return pl.pallas_call(
         finish_kernel,
         out_shape=shapes,
-        in_specs=[anywhere] * 3,
+        in_specs=[pl.BlockSpec(memory_space=pltpu.VMEM)] * 3,
         out_specs=(hbm, hbm, hbm),
         scratch_shapes=[dma((3,))],
+        compiler_params=pltpu.CompilerParams(vmem_limit_bytes=8 << 20),
         name="finish",
     )(*results)
 

time: 49.2 us -> 28.6 us (0.58); the launches traced: 48.5 us -> 28.5 us
  Pallas kernels: 47.2 us -> 27.2 us
    pallas_call x2, Pallas kernels: 47.2 us -> 27.2 us  [the longest x1 26.4 us: per_device(): pl.pallas_call(window_kernel, out_shape=tuple((pltpu.VMEM(x.shape, x.dtyp...]
where the time goes in v4:
time: 28.6 us; the launch traced here: 28.5 us
  Pallas kernels  27.2 us (95%)
  between operations  1.29 us (5%)
    pallas_call x1, Pallas kernels, per_device(): pl.pallas_call(window_kernel, out_shape=tuple((pltpu.VMEM(x.shape, x.dtyp...  26.4 us
    pallas_call x1, Pallas kernels, per_device(): pl.pallas_call(finish_kernel, out_shape=shapes, in_specs=[pl.BlockSpec(me...  0.86 us

profile of v4, /device:TPU:97, one launch (start us, length us, event | category | flops | bytes accessed | tf_op | source)
XLA Modules:
  0.0 28.5 jit_solution(2828215926573147682)
XLA Ops:
  1.3 26.4 %window.1 = (f32[32,8,128]{2,1,0:T(8,128)S(1)}, bf16[64,8,256]{2,1,0:T(8,128)(2,1)S(1)}, bf16[64,8,256]{2,1,0:T(8,128)(2,1)S(1)}) custom-call(s32[1]{0:T(128)S(6)} %copy.14.n_ref, f32[64]{0:T(128)} %nu_hbm.1, s32[2,32]{1,0:T(2,128)} %bitcast.11, s32[2,32]{1,0:T(2,128)} %bitcast.12, s32[2,32]{1,0:T(2,128)} %bitcast.13, f32[32,8,128]{2,1,0:T(8,128)} %force_hbm.1, ...), custom_call_target="tpu_custom_call" | custom-call | tf_op jit(solution)/shard_map/window/pallas_call | solution.py:446
  27.7 0.9 %finish.1 = (f32[32,8,128]{2,1,0:T(8,128)}, bf16[64,8,256]{2,1,0:T(8,128)(2,1)}, bf16[64,8,256]{2,1,0:T(8,128)(2,1)}) custom-call(f32[32,8,128]{2,1,0:T(8,128)S(1)} %get-tuple-element.6.ocean_in, bf16[64,8,256]{2,1,0:T(8,128)(2,1)S(1)} %get-tuple-element.7.u_in, bf16[64,8,256]{2,1,0:T(8,128)(2,1)S(1)} %get-tuple-element.8.v_in), custom_call_target="tpu_custom_call" | custom-call | tf_op jit(solution)/shard_map/finish/pallas_call | solution.py:518

commit v5 on v4

--- a/solution.py
+++ b/solution.py
@@ -76,7 +76,7 @@
     def transform(t):
         for part in range(2):
             at = part * K + t * KT
-            raw[t, part] = jnp.dot(packed[...], table[:, at : at + KT], preferred_element_type=jnp.float32)
+            raw[t, part, 0:total, :] = jnp.dot(packed[0:total, :], table[:, at : at + KT], preferred_element_type=jnp.float32)
 
     def twist(t):
         cos_at, sin_at = slice(t * KT, (t + 1) * KT), slice(K + t * KT, K + (t + 1) * KT)
@@ -107,6 +107,10 @@
         result[here] = jnp.dot(spread[here], table_t[...], preferred_element_type=jnp.float32)
 
 
+def wrapped(index, count):
+    return jnp.where(index >= count, index - count, index)
+
+
 def shift_rows(cells, down, edge):
     row = lax.broadcasted_iota(jnp.int32, cells.shape, 0)
     last = cells.shape[0] - 1
@@ -129,9 +133,9 @@
     nu_ref, src_ref, dst_ref, live_ref, force, mix, mask, weight, last_u, load_sem,
     cells, ratio, ocean, send_n, send_s, send_w, send_e, got_n, got_s, got_w, got_e, halo_send, halo_recv,
     flux, note, notes, note_send, note_recv,
-    stage, got_u, got_v, fwd_send, fwd_recv,
+    stage, got_v, got_even, got_odd, fwd_send, fwd_recv,
     coarse, fine, coarse_t, fine_t, table, table_t, twiddle,
-    packed, raw, spread, result, back_u, back_v, blank, back_send, back_recv, ocean_sem,
+    packed, raw, spread, result, back_v, back_even, back_odd, blank, back_send, back_recv, ocean_sem,
 ):
     me, oc = lax.axis_index("lon"), lax.axis_index("ocn")
     n_lon, n_ocn = lax.axis_size("lon"), lax.axis_size("ocn")
@@ -139,6 +143,7 @@
     last_owner = n_lon - 1
     share = 2
     source = me < NBLK
+    start_at = wrapped(me, NBLK)
 
     def mine(t):
         return pl.ds(share * t, share)
@@ -148,7 +153,7 @@
         pltpu.make_async_copy(mix_hbm, mix, load_sem.at[1]),
         pltpu.make_async_copy(mask_hbm, mask, load_sem.at[2]),
         pltpu.make_async_copy(weight_hbm.at[pl.ds(0, NBLK)], weight, load_sem.at[3]),
-        pltpu.make_async_copy(u_hbm.at[mine(last_owner)], last_u, load_sem.at[4]),
+        pltpu.make_async_copy(u_hbm.at[pl.ds(share * n_lon - 1, 1)], last_u, load_sem.at[4]),
         pltpu.make_async_copy(nu_hbm, nu_ref, load_sem.at[5]),
         pltpu.make_async_copy(src_hbm, src_ref, load_sem.at[6]),
         pltpu.make_async_copy(dst_hbm, dst_ref, load_sem.at[7]),
@@ -160,7 +165,7 @@
     barrier = pltpu.get_barrier_semaphore()
 
     def greet(i, carry):
-        pl.semaphore_signal(barrier, inc=1, device_id={"lon": lax.rem(me + i, n_lon)}, device_id_type=MESH)
+        pl.semaphore_signal(barrier, inc=1, device_id={"lon": wrapped(me + i, n_lon)}, device_id_type=MESH)
         return carry
 
     lax.fori_loop(1, n_lon, greet, 0)
@@ -172,6 +177,9 @@
     @pl.when(oc < n_ocn - 1)
     def _():
         pl.semaphore_signal(barrier, inc=1, device_id={"ocn": oc + 1}, device_id_type=MESH)
+
+    points = n_ref[0].astype(jnp.float32)
+    build_tables(points, coarse, fine, coarse_t, fine_t, table, table_t, twiddle)
 
     for load in loads[:3]:
         load.wait()
@@ -226,30 +234,39 @@
         def _(into=into):
             into[...] = jnp.zeros_like(into)
 
-    def send_rows(f, field, got):
+    groups = (
+        (v_hbm, 0, 2, got_v, back_v, out_v, 0),
+        (u_hbm, 0, 1, got_even, back_even, out_u, 1),
+        (u_hbm, 1, 1, got_odd, back_odd, out_u, 1),
+    )
+
+    def send_rows(g):
+        field, first, depth, got = groups[g][:4]
+
+        def rows_of(t):
+            return field.at[pl.ds(share * t + first, depth)]
+
         def forward(i, carry):
-            t = lax.rem(me + i, n_lon)
+            t = wrapped(me + i, n_lon)
 
             def start():
                 pltpu.make_async_remote_copy(
-                    src_ref=field.at[mine(t)], dst_ref=got.at[me], send_sem=fwd_send.at[f], recv_sem=fwd_recv.at[f], device_id={"lon": t}, device_id_type=MESH
+                    src_ref=rows_of(t), dst_ref=got.at[me], send_sem=fwd_send.at[g], recv_sem=fwd_recv.at[g], device_id={"lon": t}, device_id_type=MESH
                 ).start()
 
-            if f == 0:
+            if g < 2:
                 start()
             else:
                 pl.when(t != last_owner)(start)
             return carry
 
-        @pl.when(source)
-        def _():
-            lax.fori_loop(1, n_lon, forward, 0)
-            pltpu.make_async_copy(field.at[mine(me)], got.at[me], fwd_recv.at[f]).start()
-
-    send_rows(0, v_hbm, got_v)
-
-    points = n_ref[0].astype(jnp.float32)
-    build_tables(points, coarse, fine, coarse_t, fine_t, table, table_t, twiddle)
+        lax.fori_loop(1, n_lon, forward, 0, unroll=4)
+        pltpu.make_async_copy(rows_of(me), got.at[me], fwd_recv.at[g]).start()
+
+    @pl.when(source)
+    def _():
+        for g in range(2):
+            send_rows(g)
 
     for i in range(4):
         has, gets, into, copy = halo(i)
@@ -288,9 +305,11 @@
         note[p] = jnp.where(row < 2, got, codes)[0:4]
         return carry
 
-    lax.fori_loop(0, NBLK, owner, 0, unroll=3)
-
-    def tell(p, carry):
+    lax.fori_loop(0, NBLK, owner, 0, unroll=21)
+
+    def tell(i, carry):
+        p = wrapped(start_at + i, NBLK)
+
         @pl.when(p != me)
         def _():
             pltpu.make_async_remote_copy(
@@ -299,21 +318,20 @@
 
         return carry
 
-    lax.fori_loop(0, NBLK, tell, 0)
+    lax.fori_loop(0, NBLK, tell, 0, unroll=3)
 
     @pl.when(source)
     def _():
         pltpu.make_async_copy(note.at[me], notes.at[me], note_recv).start()
-
-    send_rows(1, u_hbm, got_u)
+        send_rows(2)
+
     for z in range(1, levels):
         ocean[z] = mixed(z)
     ocean_copy = pltpu.make_async_copy(ocean, out_ocean, ocean_sem)
     ocean_copy.start()
     loads[4].wait()
 
-    @pl.when(source)
-    def _():
+    def couple():
         pltpu.make_async_copy(notes, notes, note_recv).wait()
         even = 2.0 * iota((8, BLK), 0)
         odd = even + 1.0
@@ -330,60 +348,68 @@
         blank_sum = jnp.zeros((8, BLK), jnp.float32)
         sum_even, sum_odd = lax.fori_loop(0, n_lon, add, (blank_sum, blank_sum), unroll=4)
         coupling = jnp.concatenate([sum_even, sum_odd], 1)
-        stage[0] = last_u[0]
-        stage[1] = (last_u[1].astype(jnp.float32) + coupling).astype(jnp.bfloat16)
+        stage[0] = (last_u[0].astype(jnp.float32) + coupling).astype(jnp.bfloat16)
         pltpu.make_async_remote_copy(
-            src_ref=stage, dst_ref=got_u.at[me], send_sem=fwd_send.at[1], recv_sem=fwd_recv.at[1], device_id={"lon": last_owner}, device_id_type=MESH
+            src_ref=stage, dst_ref=got_odd.at[me], send_sem=fwd_send.at[2], recv_sem=fwd_recv.at[2], device_id={"lon": last_owner}, device_id_type=MESH
         ).start()
 
     loads[5].wait()
-    column = iota((16, SEGLON), 1)
-    row = iota((16, KT), 0)
-    nu = jnp.where(row < 8, nu_ref[share * me], nu_ref[share * me + 1])
-    for f, (got, back, out) in enumerate(((got_v, back_v, out_v), (got_u, back_u, out_u))):
-        pltpu.make_async_copy(got, got, fwd_recv.at[f]).wait()
-
-        def pack(l, carry, got=got):
+    for g, (field, first, depth, got, back, out, f) in enumerate(groups):
+        rows = 8 * depth
+        column = iota((rows, SEGLON), 1)
+        if g == 1:
+            pl.when(source)(couple)
+        pltpu.make_async_copy(got, got, fwd_recv.at[g]).wait()
+
+        def pack(l, carry, got=got, rows=rows, column=column):
             inside = column + (l * SEGLON).astype(jnp.float32) < points
-            block = got[l].astype(jnp.float32).reshape(16, SEGLON)
-            packed[pl.ds(pl.multiple_of(16 * l, 16), 16), :] = jnp.where(inside, block, 0.0).astype(jnp.bfloat16)
+            block = got[l].astype(jnp.float32).reshape(rows, SEGLON)
+            result[pl.ds(pl.multiple_of(rows * l, 8), rows), :] = jnp.where(inside, block, 0.0)
             return carry
 
-        lax.fori_loop(0, NBLK, pack, 0)
-        spectral(16, points, nu, packed, table, table_t, twiddle, raw, spread, result)
-
-        def unpack(l, carry, back=back, out=out, f=f):
+        lax.fori_loop(0, NBLK, pack, 0, unroll=3)
+        total = pl.ds(0, NBLK * rows)
+        packed[total, :] = result[total, :].astype(jnp.bfloat16)
+        viscosity = nu_ref[share * me + first]
+        if depth == 2:
+            viscosity = jnp.where(lax.broadcasted_iota(jnp.int32, (rows, KT), 0) < 8, viscosity, nu_ref[share * me + 1])
+        spectral(rows, points, viscosity, packed, table, table_t, twiddle, raw, spread, result)
+        own = pl.ds(share * me + first, depth)
+
+        def unpack(i, carry, back=back, out=out, rows=rows, depth=depth, column=column, own=own, g=g, f=f):
+            l = wrapped(start_at + i, NBLK)
             inside = column + (l * SEGLON).astype(jnp.float32) < points
-            block = result[pl.ds(pl.multiple_of(16 * l, 16), 16), :]
-            back[l] = jnp.where(inside, block, 0.0).reshape(2, 8, SEGLON).astype(jnp.bfloat16)
+            block = result[pl.ds(pl.multiple_of(rows * l, 8), rows), :]
+            back[l] = jnp.where(inside, block, 0.0).reshape(depth, 8, SEGLON).astype(jnp.bfloat16)
 
             @pl.when(l != me)
             def _():
                 pltpu.make_async_remote_copy(
-                    src_ref=back.at[l], dst_ref=out.at[mine(me)], send_sem=back_send.at[f], recv_sem=back_recv.at[f], device_id={"lon": l}, device_id_type=MESH
+                    src_ref=back.at[l], dst_ref=out.at[own], send_sem=back_send.at[g], recv_sem=back_recv.at[f], device_id={"lon": l}, device_id_type=MESH
                 ).start()
 
             return carry
 
-        lax.fori_loop(0, NBLK, unpack, 0)
+        lax.fori_loop(0, NBLK, unpack, 0, unroll=3)
 
         @pl.when(source)
-        def _(back=back, out=out, f=f):
-            pltpu.make_async_copy(back.at[me], out.at[mine(me)], back_recv.at[f]).start()
+        def _(back=back, out=out, own=own, f=f):
+            pltpu.make_async_copy(back.at[me], out.at[own], back_recv.at[f]).start()
 
         @pl.when(jnp.logical_not(source))
-        def _(back=back, out=out, f=f):
-            if f == 0:
+        def _(out=out, g=g, f=f):
+            if g == 0:
                 blank[...] = jnp.zeros_like(blank)
-            pltpu.make_async_copy(blank, out, back_recv.at[f]).start()
+            if g < 2:
+                pltpu.make_async_copy(blank, out, back_recv.at[f]).start()
 
     ocean_copy.wait()
 
     @pl.when(source)
     def _():
-        for f in range(2):
-            sent = v_hbm.at[pl.ds(0, share * (n_lon - 1))]
-            pltpu.make_async_copy(sent, sent, fwd_send.at[f]).wait()
+        for g, (field, first, depth, got, back, out, f) in enumerate(groups):
+            sent = field.at[pl.ds(0, depth * (n_lon - 1))]
+            pltpu.make_async_copy(sent, sent, fwd_send.at[g]).wait()
         told = note.at[pl.ds(0, NBLK - 1)]
         pltpu.make_async_copy(told, told, note_send).wait()
 
@@ -391,17 +417,18 @@
     def _():
         pltpu.make_async_copy(note, note, note_send).wait()
 
-    for f, (back, out) in enumerate(((back_v, out_v), (back_u, out_u))):
+    for g, (field, first, depth, got, back, out, f) in enumerate(groups):
 
         @pl.when(source)
-        def _(back=back, f=f):
+        def _(back=back, g=g):
             sent = back.at[pl.ds(0, NBLK - 1)]
-            pltpu.make_async_copy(sent, sent, back_send.at[f]).wait()
+            pltpu.make_async_copy(sent, sent, back_send.at[g]).wait()
 
         @pl.when(jnp.logical_not(source))
-        def _(back=back, f=f):
-            pltpu.make_async_copy(back, back, back_send.at[f]).wait()
-
+        def _(back=back, g=g):
+            pltpu.make_async_copy(back, back, back_send.at[g]).wait()
+
+    for f, out in enumerate((out_v, out_u)):
         pltpu.make_async_copy(out, out, back_recv.at[f]).wait()
 
 
@@ -436,6 +463,7 @@
     smem = pl.BlockSpec(memory_space=pltpu.SMEM)
     hbm = pl.BlockSpec(memory_space=pltpu.HBM)
     anywhere = pl.BlockSpec(memory_space=pl.ANY)
+    one = (1,) + atm_u.shape[1:]
     two = (2,) + atm_u.shape[1:]
     edge = (levels + 8, BLK)
     shapes = (
@@ -457,7 +485,7 @@
             pltpu.VMEM(mixing_coef.shape, f32),
             pltpu.VMEM(land_mask.shape, jnp.int32),
             pltpu.VMEM((NBLK, slots[1], BLK, BLK), bf16),
-            pltpu.VMEM(two, bf16),
+            pltpu.VMEM(one, bf16),
             dma((9,)),
             pltpu.VMEM((levels + 1,) + tile, f32),
             pltpu.VMEM((levels,) + tile, f32),
@@ -477,11 +505,12 @@
             pltpu.VMEM((lon_devices, 4, BLK), f32),
             dma,
             dma,
-            pltpu.VMEM(two, bf16),
+            pltpu.VMEM(one, bf16),
             pltpu.VMEM((NBLK,) + two, bf16),
-            pltpu.VMEM((NBLK,) + two, bf16),
-            dma((2,)),
-            dma((2,)),
+            pltpu.VMEM((NBLK,) + one, bf16),
+            pltpu.VMEM((NBLK,) + one, bf16),
+            dma((3,)),
+            dma((3,)),
             pltpu.VMEM((2, 16, K), f32),
             pltpu.VMEM((2, 16, K), f32),
             pltpu.VMEM((2, K // 16, SEGLON), f32),
@@ -494,9 +523,10 @@
             pltpu.VMEM((m, 2 * K), bf16),
             pltpu.VMEM((m, SEGLON), f32),
             pltpu.VMEM((NBLK,) + two, bf16),
-            pltpu.VMEM((NBLK,) + two, bf16),
+            pltpu.VMEM((NBLK,) + one, bf16),
+            pltpu.VMEM((NBLK,) + one, bf16),
             pltpu.VMEM(atm_u.shape, bf16),
-            dma((2,)),
+            dma((3,)),
             dma((2,)),
             dma,
         ],

time: 28.6 us -> 27.2 us (0.951)
  Pallas kernels: 27.2 us -> 25.8 us
    pallas_call x1, Pallas kernels: 26.4 us -> 24.9 us  [per_device(): pl.pallas_call(window_kernel, out_shape=tuple((pltpu.VMEM(x.shape, x.dtyp...]
where the time goes in v5:
time: 27.2 us; the launch traced here: 27.1 us
  Pallas kernels  25.8 us (95%)
  between operations  1.29 us (5%)
    pallas_call x1, Pallas kernels, per_device(): pl.pallas_call(window_kernel, out_shape=tuple((pltpu.VMEM(x.shape, x.dtyp...  24.9 us
    pallas_call x1, Pallas kernels, per_device(): pl.pallas_call(finish_kernel, out_shape=shapes, in_specs=[pl.BlockSpec(me...  0.86 us

profile of v5, /device:TPU:97, one launch (start us, length us, event | category | flops | bytes accessed | tf_op | source)
XLA Modules:
  0.0 27.1 jit_solution(12206990041844107584)
XLA Ops:
  1.3 24.9 %window.1 = (f32[32,8,128]{2,1,0:T(8,128)S(1)}, bf16[64,8,256]{2,1,0:T(8,128)(2,1)S(1)}, bf16[64,8,256]{2,1,0:T(8,128)(2,1)S(1)}) custom-call(s32[1]{0:T(128)S(6)} %copy.14.n_ref, f32[64]{0:T(128)} %nu_hbm.1, s32[2,32]{1,0:T(2,128)} %bitcast.11, s32[2,32]{1,0:T(2,128)} %bitcast.12, s32[2,32]{1,0:T(2,128)} %bitcast.13, f32[32,8,128]{2,1,0:T(8,128)} %force_hbm.1, ...), custom_call_target="tpu_custom_call" | custom-call | tf_op jit(solution)/shard_map/window/pallas_call | solution.py:474
  26.2 0.9 %finish.1 = (f32[32,8,128]{2,1,0:T(8,128)}, bf16[64,8,256]{2,1,0:T(8,128)(2,1)}, bf16[64,8,256]{2,1,0:T(8,128)(2,1)}) custom-call(f32[32,8,128]{2,1,0:T(8,128)S(1)} %get-tuple-element.6.ocean_in, bf16[64,8,256]{2,1,0:T(8,128)(2,1)S(1)} %get-tuple-element.7.u_in, bf16[64,8,256]{2,1,0:T(8,128)(2,1)S(1)} %get-tuple-element.8.v_in), custom_call_target="tpu_custom_call" | custom-call | tf_op jit(solution)/shard_map/finish/pallas_call | solution.py:548

commit v6 on v5

--- a/solution.py
+++ b/solution.py
@@ -107,6 +107,9 @@
         result[here] = jnp.dot(spread[here], table_t[...], preferred_element_type=jnp.float32)
 
 
+STEPS = [((2, 1, 3, 0)[(a + b) % 4], (2, 1, 3, 0)[b], core) for a in range(4) for b in range(4) for core in range(2)]
+
+
 def wrapped(index, count):
     return jnp.where(index >= count, index - count, index)
 
@@ -144,6 +147,14 @@
     share = 2
     source = me < NBLK
     start_at = wrapped(me, NBLK)
+    x, y, core = me // 8, lax.rem(me // 2, 4), lax.rem(me, 2)
+    x_at = [8 * wrapped(x + d, 4) for d in range(4)]
+    y_at = [2 * wrapped(y + d, 4) for d in range(4)]
+    c_at = [core, 1 - core]
+
+    def peer(step):
+        return x_at[step[0]] + y_at[step[1]] + c_at[step[2]]
+
 
     def mine(t):
         return pl.ds(share * t, share)
@@ -159,16 +170,10 @@
         pltpu.make_async_copy(dst_hbm, dst_ref, load_sem.at[7]),
         pltpu.make_async_copy(live_hbm, live_ref, load_sem.at[8]),
     ]
-    for load in loads:
-        load.start()
-
     barrier = pltpu.get_barrier_semaphore()
-
-    def greet(i, carry):
-        pl.semaphore_signal(barrier, inc=1, device_id={"lon": wrapped(me + i, n_lon)}, device_id_type=MESH)
-        return carry
-
-    lax.fori_loop(1, n_lon, greet, 0)
+    for step in STEPS:
+        if step != (0, 0, 0):
+            pl.semaphore_signal(barrier, inc=1, device_id={"lon": peer(step)}, device_id_type=MESH)
 
     @pl.when(oc > 0)
     def _():
@@ -178,8 +183,8 @@
     def _():
         pl.semaphore_signal(barrier, inc=1, device_id={"ocn": oc + 1}, device_id_type=MESH)
 
-    points = n_ref[0].astype(jnp.float32)
-    build_tables(points, coarse, fine, coarse_t, fine_t, table, table_t, twiddle)
+    for load in loads:
+        load.start()
 
     for load in loads[:3]:
         load.wait()
@@ -246,27 +251,27 @@
         def rows_of(t):
             return field.at[pl.ds(share * t + first, depth)]
 
-        def forward(i, carry):
-            t = wrapped(me + i, n_lon)
-
-            def start():
-                pltpu.make_async_remote_copy(
-                    src_ref=rows_of(t), dst_ref=got.at[me], send_sem=fwd_send.at[g], recv_sem=fwd_recv.at[g], device_id={"lon": t}, device_id_type=MESH
-                ).start()
-
+        for step in STEPS:
+            if step == (0, 0, 0):
+                continue
+            t = peer(step)
+            copy = pltpu.make_async_remote_copy(
+                src_ref=rows_of(t), dst_ref=got.at[me], send_sem=fwd_send.at[g], recv_sem=fwd_recv.at[g], device_id={"lon": t}, device_id_type=MESH
+            )
             if g < 2:
-                start()
+                copy.start()
             else:
-                pl.when(t != last_owner)(start)
-            return carry
-
-        lax.fori_loop(1, n_lon, forward, 0, unroll=4)
+                pl.when(t != last_owner)(copy.start)
+
         pltpu.make_async_copy(rows_of(me), got.at[me], fwd_recv.at[g]).start()
 
     @pl.when(source)
     def _():
         for g in range(2):
             send_rows(g)
+
+    points = n_ref[0].astype(jnp.float32)
+    build_tables(points, coarse, fine, coarse_t, fine_t, table, table_t, twiddle)
 
     for i in range(4):
         has, gets, into, copy = halo(i)
@@ -376,21 +381,23 @@
         spectral(rows, points, viscosity, packed, table, table_t, twiddle, raw, spread, result)
         own = pl.ds(share * me + first, depth)
 
-        def unpack(i, carry, back=back, out=out, rows=rows, depth=depth, column=column, own=own, g=g, f=f):
-            l = wrapped(start_at + i, NBLK)
+        def unpack(l, carry, back=back, rows=rows, depth=depth, column=column):
             inside = column + (l * SEGLON).astype(jnp.float32) < points
             block = result[pl.ds(pl.multiple_of(rows * l, 8), rows), :]
             back[l] = jnp.where(inside, block, 0.0).reshape(depth, 8, SEGLON).astype(jnp.bfloat16)
-
-            @pl.when(l != me)
-            def _():
+            return carry
+
+        lax.fori_loop(0, NBLK, unpack, 0, unroll=7)
+        for step in STEPS:
+            if step == (0, 0, 0):
+                continue
+            l = peer(step)
+
+            @pl.when(l < NBLK)
+            def _(l=l, back=back, out=out, own=own, g=g, f=f):
                 pltpu.make_async_remote_copy(
                     src_ref=back.at[l], dst_ref=out.at[own], send_sem=back_send.at[g], recv_sem=back_recv.at[f], device_id={"lon": l}, device_id_type=MESH
                 ).start()
-
-            return carry
-
-        lax.fori_loop(0, NBLK, unpack, 0, unroll=3)
 
         @pl.when(source)
         def _(back=back, out=out, own=own, f=f):

time: 27.2 us -> 26.6 us (0.978)
  Pallas kernels: 25.8 us -> 25.2 us
    pallas_call x1, Pallas kernels: 24.9 us -> 24.3 us  [per_device(): pl.pallas_call(window_kernel, out_shape=tuple((pltpu.VMEM(x.shape, x.dtyp...]
where the time goes in v6:
time: 26.6 us; the launch traced here: 26.5 us
  Pallas kernels  25.2 us (95%)
  between operations  1.29 us (5%)
    pallas_call x1, Pallas kernels, per_device(): pl.pallas_call(window_kernel, out_shape=tuple((pltpu.VMEM(x.shape, x.dtyp...  24.3 us
    pallas_call x1, Pallas kernels, per_device(): pl.pallas_call(finish_kernel, out_shape=shapes, in_specs=[pl.BlockSpec(me...  0.86 us

profile of v6, /device:TPU:97, one launch (start us, length us, event | category | flops | bytes accessed | tf_op | source)
XLA Modules:
  0.0 26.5 jit_solution(4114113714601380092)
XLA Ops:
  1.3 24.3 %window.1 = (f32[32,8,128]{2,1,0:T(8,128)S(1)}, bf16[64,8,256]{2,1,0:T(8,128)(2,1)S(1)}, bf16[64,8,256]{2,1,0:T(8,128)(2,1)S(1)}) custom-call(s32[1]{0:T(128)S(6)} %copy.14.n_ref, f32[64]{0:T(128)} %nu_hbm.1, s32[2,32]{1,0:T(2,128)} %bitcast.11, s32[2,32]{1,0:T(2,128)} %bitcast.12, s32[2,32]{1,0:T(2,128)} %bitcast.13, f32[32,8,128]{2,1,0:T(8,128)} %force_hbm.1, ...), custom_call_target="tpu_custom_call" | custom-call | tf_op jit(solution)/shard_map/window/pallas_call | solution.py:481
  25.6 0.9 %finish.1 = (f32[32,8,128]{2,1,0:T(8,128)}, bf16[64,8,256]{2,1,0:T(8,128)(2,1)}, bf16[64,8,256]{2,1,0:T(8,128)(2,1)}) custom-call(f32[32,8,128]{2,1,0:T(8,128)S(1)} %get-tuple-element.6.ocean_in, bf16[64,8,256]{2,1,0:T(8,128)(2,1)S(1)} %get-tuple-element.7.u_in, bf16[64,8,256]{2,1,0:T(8,128)(2,1)S(1)} %get-tuple-element.8.v_in), custom_call_target="tpu_custom_call" | custom-call | tf_op jit(solution)/shard_map/finish/pallas_call | solution.py:555

commit v7 on v6

--- a/solution.py
+++ b/solution.py
@@ -312,18 +312,16 @@
 
     lax.fori_loop(0, NBLK, owner, 0, unroll=21)
 
-    def tell(i, carry):
-        p = wrapped(start_at + i, NBLK)
-
-        @pl.when(p != me)
-        def _():
+    for step in STEPS:
+        if step == (0, 0, 0):
+            continue
+        p = peer(step)
+
+        @pl.when(p < NBLK)
+        def _(p=p):
             pltpu.make_async_remote_copy(
                 src_ref=note.at[p], dst_ref=notes.at[me], send_sem=note_send, recv_sem=note_recv, device_id={"lon": p}, device_id_type=MESH
             ).start()
-
-        return carry
-
-    lax.fori_loop(0, NBLK, tell, 0, unroll=3)
 
     @pl.when(source)
     def _():

time: 26.6 us -> 26.7 us (level)
  no operation moved by 1% of the time
where the time goes in v7:
time: 26.7 us; the launch traced here: 26.6 us
  Pallas kernels  25.3 us (95%)
  between operations  1.29 us (5%)
    pallas_call x1, Pallas kernels, per_device(): pl.pallas_call(window_kernel, out_shape=tuple((pltpu.VMEM(x.shape, x.dtyp...  24.4 us
    pallas_call x1, Pallas kernels, per_device(): pl.pallas_call(finish_kernel, out_shape=shapes, in_specs=[pl.BlockSpec(me...  0.86 us

profile of v7, /device:TPU:97, one launch (start us, length us, event | category | flops | bytes accessed | tf_op | source)
XLA Modules:
  0.0 26.6 jit_solution(4725022961756063311)
XLA Ops:
  1.3 24.4 %window.1 = (f32[32,8,128]{2,1,0:T(8,128)S(1)}, bf16[64,8,256]{2,1,0:T(8,128)(2,1)S(1)}, bf16[64,8,256]{2,1,0:T(8,128)(2,1)S(1)}) custom-call(s32[1]{0:T(128)S(6)} %copy.14.n_ref, f32[64]{0:T(128)} %nu_hbm.1, s32[2,32]{1,0:T(2,128)} %bitcast.11, s32[2,32]{1,0:T(2,128)} %bitcast.12, s32[2,32]{1,0:T(2,128)} %bitcast.13, f32[32,8,128]{2,1,0:T(8,128)} %force_hbm.1, ...), custom_call_target="tpu_custom_call" | custom-call | tf_op jit(solution)/shard_map/window/pallas_call | solution.py:479
  25.7 0.9 %finish.1 = (f32[32,8,128]{2,1,0:T(8,128)}, bf16[64,8,256]{2,1,0:T(8,128)(2,1)}, bf16[64,8,256]{2,1,0:T(8,128)(2,1)}) custom-call(f32[32,8,128]{2,1,0:T(8,128)S(1)} %get-tuple-element.6.ocean_in, bf16[64,8,256]{2,1,0:T(8,128)(2,1)S(1)} %get-tuple-element.7.u_in, bf16[64,8,256]{2,1,0:T(8,128)(2,1)S(1)} %get-tuple-element.8.v_in), custom_call_target="tpu_custom_call" | custom-call | tf_op jit(solution)/shard_map/finish/pallas_call | solution.py:553
